TPU v7x, 128 devices: a whole 4x4x4 slice. The times are simulated.
128 devices in a mesh: shard: 32 (over y, z, core), tensor: 4 (over x).
Axes of the slice: x: 4, y: 4, z: 4, core: 2. Of those that a mesh axis runs over, the one named last changes fastest.
Arguments:
- gradient: float32 [384, 4, 20736], P('shard', 'tensor'), may hold values from -6 to 6
- weight: float32 [384, 4, 20736], P('shard', 'tensor'), may hold values from -0.3125 to 0.3125
- first_moment: float32 [384, 4, 20736], P('shard', 'tensor'), may hold values from -6 to 6
- second_moment: float32 [384, 4, 20736], P('shard', 'tensor'), may hold values from 0.3 to 3
- left_basis: float32 [384, 4, 5760], P('shard', 'tensor')
- left_gram: float32 [384, 4, 5760], P('shard', 'tensor'), as said below
- owner_table: int32 [12, 5], replicated, may hold values from 0 to 31, as said below
- bias_gradient: float32 [69120], P(('shard', 'tensor')), may hold values from -6 to 6
- bias_weight: float32 [69120], P(('shard', 'tensor')), may hold values from -3 to 3
- bias_first: float32 [69120], P(('shard', 'tensor')), may hold values from -6 to 6
- bias_second: float32 [69120], P(('shard', 'tensor')), may hold values from 0.3 to 3
Outputs:
- new_weight: float32 [384, 4, 20736], P('shard', 'tensor')
- new_first: float32 [384, 4, 20736], P('shard', 'tensor')
- new_second: float32 [384, 4, 20736], P('shard', 'tensor')
- owned_basis: float32 [32, 2, 384, 384], P('shard', None, None, 'tensor')
- owned_gram: float32 [32, 2, 384, 384], P('shard', None, None, 'tensor')
- bias_updated: float32 [69120], P(('shard', 'tensor'))
- bias_first_new: float32 [69120], P(('shard', 'tensor'))
- bias_second_new: float32 [69120], P(('shard', 'tensor'))
Inputs may be any that keep to these rules, and one draw needn't show every extreme that they name: `owner_table`: every owner group that owns a matrix owns exactly 2, with at most 8 column tiles together, and some group has exactly 8; group 0 and the last group own matrices. `left_gram`: each matrix is symmetric.
All inputs are finite; a program needn't handle non-finite values.
Results may differ from a plain program's by a relative error of at most 0.0001.
Values sent between devices are 32-bit elements; how exact they have to be, the bound alone decides.
A program may use at most 128 MiB of HBM per device.

v0:
```python
import functools

import jax
import jax.numpy as jnp
from jax import lax
from jax.experimental import pallas as pl
from jax.experimental.pallas import tpu as pltpu
from jax.sharding import PartitionSpec as P

MESH = pl.DeviceIdType.MESH
STEP = 10
NS_STEPS = 5
N_SHARD = 32
N_TENSOR = 4
D = 384
ROWS = 12
PAIRS = 6
TYPE_TILES = (3, 1, 4, 4, 6)
TYPE_START = (0, 3, 4, 8, 12)
TYPE_CHUNKS = (3, 1, 3, 3, 5)
CHUNK_START = (0, 3, 4, 7, 10)
CAP = 6
MSG = ROWS * CAP
QMSG = ROWS * 2
LINE = 162
QLINE = 45
ZERO_CHUNK = 180
ZERO_MAT = 60
CORR_ONE = 1.0 - 0.9**STEP
CORR_TWO = 1.0 - 0.95**STEP
TAB_M = 256
TAB_LOC = 320
TAB_C0 = 384
TAB_SIZE = 512
F32 = jnp.float32
BF16 = jnp.bfloat16


def table_kernel(owner_ref, tab_ref):
    @pl.loop(0, 256)
    def _(i):
        tab_ref[i] = ZERO_CHUNK

    @pl.loop(0, 64)
    def _(i):
        tab_ref[TAB_M + i] = ZERO_MAT

    @pl.loop(0, 32)
    def _(i):
        tab_ref[TAB_C0 + i] = 0

    @pl.loop(0, 12)
    def _(layer):
        for kind in range(5):
            mat = layer * 5 + kind
            owner = owner_ref[layer, kind]
            first = tab_ref[TAB_M + 2 * owner] == ZERO_MAT
            chunks = TYPE_CHUNKS[kind]
            held = tab_ref[TAB_C0 + owner]
            base = jnp.where(first, 0, held)
            tab_ref[TAB_M + 2 * owner + jnp.where(first, 0, 1)] = mat
            tab_ref[TAB_C0 + owner] = jnp.where(first, chunks, held)
            tab_ref[TAB_LOC + mat] = MSG * owner + base
            for j in range(chunks):
                tab_ref[owner * 8 + base + j] = layer * 15 + CHUNK_START[kind] + j


def align_rows(src, dst):
    lane = lax.broadcasted_iota(jnp.int32, (ROWS, 128), 1)

    @pl.loop(0, PAIRS)
    def _(pair):
        for half in range(2):
            for kind in range(5):
                for j in range(TYPE_CHUNKS[kind]):
                    col = 1728 * half + 96 * TYPE_START[kind] + 128 * j
                    at, shift = divmod(col, 128)
                    valid = min(128, 96 * TYPE_TILES[kind] - 128 * j)
                    val = src[pl.ds(27 * pair + at, ROWS, stride=LINE), :]
                    if shift:
                        val = pltpu.roll(val, 128 - shift, 1)
                        if valid > 128 - shift:
                            nxt = src[pl.ds(27 * pair + at + 1, ROWS, stride=LINE), :]
                            nxt = pltpu.roll(nxt, 128 - shift, 1)
                            val = jnp.where(lane < 128 - shift, val, nxt)
                    if valid < 128:
                        val = jnp.where(lane < valid, val, 0.0)
                    dst[30 * pair + 15 * half + CHUNK_START[kind] + j] = val


def align_mats(src, dst):
    lane = lax.broadcasted_iota(jnp.int32, (ROWS, 128), 1)

    @pl.loop(0, 15)
    def _(quad):
        for part in range(4):
            at, shift = divmod(96 * part, 128)
            val = src[pl.ds(3 * quad + at, ROWS, stride=QLINE), :]
            if shift:
                val = pltpu.roll(val, 128 - shift, 1)
                if 96 > 128 - shift:
                    nxt = src[pl.ds(3 * quad + at + 1, ROWS, stride=QLINE), :]
                    nxt = pltpu.roll(nxt, 128 - shift, 1)
                    val = jnp.where(lane < 128 - shift, val, nxt)
            dst[4 * quad + part] = jnp.where(lane < 96, val, 0.0)


def split(x):
    high = x.astype(BF16)
    return high, (x - high.astype(F32)).astype(BF16)


def dot3(a, b, dims):
    ah, al = a
    bh, bl = b
    dot = functools.partial(
        lax.dot_general, dimension_numbers=(dims, ((), ())), preferred_element_type=F32
    )
    return dot(ah, bh) + (dot(ah, bl) + dot(al, bh))


NN = ((1,), (0,))
NT = ((1,), (1,))


def main_kernel(
    tab,
    g_hbm,
    m_hbm,
    v_hbm,
    q_hbm,
    s_hbm,
    back_d,
    back_n,
    basis_out,
    gram_out,
    g2,
    m2,
    v2,
    q2,
    s2,
    lined,
    lined_q,
    send_g,
    send_m,
    send_v,
    send_q,
    send_s,
    recv_g,
    recv_m,
    recv_v,
    recv_s,
    qx,
    ret_d,
    ret_n,
    gram,
    xg,
    power,
    q_hi,
    q_lo,
    qt_hi,
    qt_lo,
    g_hat,
    m_hat,
    in_sem,
    send_sem,
    recv_sem,
    own_sem,
):
    me = lax.axis_index("shard")
    rank = lax.axis_index("tensor")
    my_y, my_z, my_c = me // 8, (me // 2) % 4, me % 2

    loads = []
    for n, (src, dst) in enumerate(
        ((q_hbm, q2), (g_hbm, g2), (s_hbm, s2), (m_hbm, m2), (v_hbm, v2))
    ):
        load = pltpu.make_async_copy(src, dst, in_sem.at[n])
        load.start()
        loads.append(load)

    def peer(t):
        o = (11 * t) % 32
        return (
            ((my_y + o // 8) % 4) * 8 + ((my_z + (o // 2) % 4) % 4) * 2 + (my_c + o % 2) % 2
        )

    barrier = pltpu.get_barrier_semaphore()

    @pl.loop(1, N_SHARD)
    def _(t):
        pl.semaphore_signal(barrier, inc=1, device_id=(peer(t), rank), device_id_type=MESH)

    for dx in range(1, N_TENSOR):
        pl.semaphore_signal(
            barrier, inc=1, device_id=(me, (rank + dx) % N_TENSOR), device_id_type=MESH
        )

    lined[ZERO_CHUNK] = jnp.zeros((ROWS, 128), F32)
    lined_q[ZERO_MAT] = jnp.zeros((ROWS, 128), F32)

    def exchange(send, recv, rows, n):
        def one(t):
            dst = peer(t)
            return pltpu.make_async_remote_copy(
                src_ref=send.at[pl.ds(pl.multiple_of(dst * rows, 8), rows)],
                dst_ref=recv.at[pl.ds(pl.multiple_of(me * rows, 8), rows)],
                send_sem=send_sem.at[n],
                recv_sem=recv_sem.at[n],
                device_id=(dst, rank),
                device_id_type=MESH,
            )

        @pl.loop(1, N_SHARD)
        def _(t):
            one(t).start()

        own = pl.ds(pl.multiple_of(me * rows, 8), rows)
        pltpu.make_async_copy(send.at[own], recv.at[own], own_sem.at[n]).start()

    def exchange_done(send, recv, rows, n):
        whole = pl.ds(0, (N_SHARD - 1) * rows)
        every = pltpu.make_async_remote_copy(
            src_ref=send.at[whole],
            dst_ref=recv.at[whole],
            send_sem=send_sem.at[n],
            recv_sem=recv_sem.at[n],
            device_id=((me + 1) % N_SHARD, rank),
            device_id_type=MESH,
        )
        own = pl.ds(pl.multiple_of(me * rows, 8), rows)
        pltpu.make_async_copy(send.at[own], recv.at[own], own_sem.at[n]).wait()
        every.wait_send()
        every.wait_recv()

    def pack(lines, send):
        @pl.loop(0, N_SHARD)
        def _(d):
            for k in range(CAP):
                send[pl.ds(MSG * d + k, ROWS, stride=CAP), :] = lines[tab[d * 8 + k]]

    def pack_mats(lines, send):
        @pl.loop(0, N_SHARD)
        def _(d):
            for j in range(2):
                send[pl.ds(QMSG * d + j, ROWS, stride=2), :] = lines[tab[TAB_M + 2 * d + j]]

    loads[0].wait()
    align_mats(q2, lined_q)
    pack_mats(lined_q, send_q)
    pl.semaphore_wait(barrier, N_SHARD - 1 + N_TENSOR - 1)
    exchange(send_q, qx.at[rank], QMSG, 0)

    loads[1].wait()
    align_rows(g2, lined)
    pack(lined, send_g)
    exchange(send_g, recv_g, MSG, 1)

    loads[2].wait()
    align_mats(s2, lined_q)
    pack_mats(lined_q, send_s)
    exchange(send_s, recv_s, QMSG, 2)

    loads[3].wait()
    m2[...] = 0.9 * m2[...] + 0.1 * g2[...]
    align_rows(m2, lined)
    pack(lined, send_m)
    exchange(send_m, recv_m, MSG, 3)

    loads[4].wait()
    align_rows(v2, lined)
    pack(lined, send_v)
    exchange(send_v, recv_v, MSG, 4)

    def spread(src_of, dst_of, n):
        for dx in range(1, N_TENSOR):
            other = (rank + dx) % N_TENSOR
            pltpu.make_async_remote_copy(
                src_ref=src_of(other),
                dst_ref=dst_of(rank),
                send_sem=send_sem.at[n],
                recv_sem=recv_sem.at[n],
                device_id=(me, other),
                device_id_type=MESH,
            ).start()

    def spread_done(three, n):
        every = pltpu.make_async_remote_copy(
            src_ref=three,
            dst_ref=three,
            send_sem=send_sem.at[n],
            recv_sem=recv_sem.at[n],
            device_id=(me, (rank + 1) % N_TENSOR),
            device_id_type=MESH,
        )
        every.wait_send()
        every.wait_recv()

    exchange_done(send_q, qx.at[rank], QMSG, 0)
    q_part = (lambda other: qx.at[rank]), (lambda other: qx.at[other])
    spread(*q_part, 5)

    exchange_done(send_g, recv_g, MSG, 1)
    c0 = tab[TAB_C0 + me]
    for j in range(2):
        left_h, left_l, right_h, right_l = [], [], [], []
        for k in range(CAP):
            chunk = recv_g[pl.ds(k, D, stride=CAP), :]
            mine = (k < c0) if j == 0 else (k >= c0)
            high, low = split(chunk)
            right_h.append(high)
            right_l.append(low)
            high, low = split(jnp.where(mine, chunk, 0.0))
            left_h.append(high)
            left_l.append(low)
        cat = functools.partial(jnp.concatenate, axis=1)
        gram[j] = dot3((cat(left_h), cat(left_l)), (cat(right_h), cat(right_l)), NT)

    def strip(x):
        return pl.ds(pl.multiple_of(96 * x, 8), 96)

    g_part = (lambda other: gram.at[:, strip(other), :]), (lambda other: xg.at[other])
    spread(*g_part, 6)

    spread_done(qx.at[pl.ds(0, 3)], 5)
    lane = lax.broadcasted_iota(jnp.int32, (D, 128), 1)
    for j in range(2):
        parts = [qx[x, pl.ds(j, D, stride=2), :] for x in range(4)]
        full = jnp.concatenate(
            [
                jnp.where(lane < 96, parts[0], pltpu.roll(parts[1], 96, 1)),
                jnp.where(lane < 64, pltpu.roll(parts[1], 96, 1), pltpu.roll(parts[2], 64, 1)),
                jnp.where(lane < 32, pltpu.roll(parts[2], 64, 1), pltpu.roll(parts[3], 32, 1)),
            ],
            axis=1,
        )
        q_hi[j], q_lo[j] = split(full)
        qt_hi[j], qt_lo[j] = split(full.T)

    exchange_done(send_s, recv_s, QMSG, 2)
    exchange_done(send_m, recv_m, MSG, 3)

    @pl.loop(0, CAP)
    def _(k):
        sel = jnp.where(k >= c0, 1, 0)
        both = jnp.concatenate(
            [recv_g[pl.ds(k, D, stride=CAP), :], recv_m[pl.ds(k, D, stride=CAP), :]], axis=1
        )
        hat = dot3((qt_hi[sel], qt_lo[sel]), split(both), NN)
        g_hat[k] = hat[:, :128]
        m_hat[k] = hat[:, 128:]

    spread_done(xg.at[pl.ds(0, 3)], 6)
    for j in range(2):
        total = gram[j, strip(rank), :]
        for dx in range(1, N_TENSOR):
            total = total + xg[(rank + dx) % N_TENSOR, j]
        held = recv_s[pl.ds(j, D, stride=2), :].T[:96]
        fresh = 0.95 * held + 0.05 * total
        gram_out[j] = fresh.T
        power[j, strip(rank), :] = dot3(split(fresh), (q_hi[j], q_lo[j]), NN)
    p_part = (
        (lambda other: power.at[:, strip(rank), :]),
        (lambda other: power.at[:, strip(other), :]),
    )
    spread(*p_part, 7)

    exchange_done(send_v, recv_v, MSG, 4)

    @pl.loop(0, CAP)
    def _(k):
        rot = g_hat[k]
        second = 0.95 * recv_v[pl.ds(k, D, stride=CAP), :] + 0.05 * rot * rot
        ret_n[pl.ds(k, D, stride=CAP), :] = second
        m_hat[k] = m_hat[k] / CORR_ONE / (jnp.sqrt(second / CORR_TWO) + 1e-08)

    exchange(ret_n, back_n, MSG, 8)

    @pl.loop(0, CAP)
    def _(k):
        sel = jnp.where(k >= c0, 1, 0)
        ret_d[pl.ds(k, D, stride=CAP), :] = dot3((q_hi[sel], q_lo[sel]), split(m_hat[k]), NN)

    exchange(ret_d, back_d, MSG, 9)

    spread_done(power.at[:, pl.ds(0, 288), :], 7)
    for j in range(2):
        full = power[j]
        norm = jnp.sqrt(jnp.sum(full * full, keepdims=True) + 1e-06)
        power[j] = full / norm

    @pl.loop(0, NS_STEPS)
    def _(sweep):
        for j in range(2):
            frame = power[j]
            pieces = split(frame)
            square = dot3(pieces, pieces, NT)
            power[j] = 1.5 * frame - 0.5 * dot3(split(square), pieces, NN)

    for x in range(N_TENSOR):

        @pl.when(rank == x)
        def _():
            basis_out[...] = power[:, :, 96 * x : 96 * x + 96]

    exchange_done(ret_n, back_n, MSG, 8)
    exchange_done(ret_d, back_d, MSG, 9)


def out_pieces():
    owner_of = []
    for half in range(2):
        for kind in range(5):
            start = 1728 * half + 96 * TYPE_START[kind]
            for c in range(96 * TYPE_TILES[kind]):
                owner_of.append((5 * half + kind, start))
    table = []
    for chunk in range(27):
        pieces = []
        for lane in range(128):
            col = 128 * chunk + lane
            mat, start = owner_of[col]
            j, src = divmod(col - start, 128)
            key = (mat, j, (lane - src) % 128)
            if pieces and pieces[-1][0] == key:
                pieces[-1][2] = lane + 1
            else:
                pieces.append([key, lane, lane + 1])
        table.append(pieces)
    return table


def unpack_kernel(tab, back_d, back_n, w2, g2, m2, weight_out, first_out, second_out):
    lane = lax.broadcasted_iota(jnp.int32, (ROWS, 128), 1)
    table = out_pieces()

    @pl.loop(0, PAIRS)
    def _(pair):
        for chunk in range(27):
            vals = [None, None]
            for (mat, j, turn), _lo, hi in reversed(table[chunk]):
                at = tab[TAB_LOC + 10 * pair + mat] + j
                for n, back in enumerate((back_d, back_n)):
                    val = back[pl.ds(at, ROWS, stride=CAP), :]
                    if turn:
                        val = pltpu.roll(val, turn, 1)
                    vals[n] = val if vals[n] is None else jnp.where(lane < hi, val, vals[n])
            here = pl.ds(27 * pair + chunk, ROWS, stride=LINE)
            w = w2[here, :]
            weight_out[here, :] = w - 0.01 * (vals[0] + 0.1 * w)
            second_out[here, :] = vals[1]

    first_out[...] = 0.9 * m2[...] + 0.1 * g2[...]


def adam_direction(moment_hat, second_new):
    return moment_hat / CORR_ONE / (jnp.sqrt(second_new / CORR_TWO) + 1e-08)


def body(
    gradient,
    weight,
    first_moment,
    second_moment,
    left_basis,
    left_gram,
    owner_table,
    bias_gradient,
    bias_weight,
    bias_first,
    bias_second,
):
    smem = pl.BlockSpec(memory_space=pltpu.SMEM)
    vmem = pl.BlockSpec(memory_space=pltpu.VMEM)
    anyw = pl.BlockSpec(memory_space=pl.ANY)
    tab = pl.pallas_call(
        table_kernel,
        out_shape=jax.ShapeDtypeStruct((TAB_SIZE,), jnp.int32),
        in_specs=[smem],
        out_specs=smem,
        name="tables",
    )(owner_table)
    flat = (ROWS * LINE, 128)
    flat_q = (ROWS * QLINE, 128)
    g, w, m, v = (a.reshape(flat) for a in (gradient, weight, first_moment, second_moment))
    q, s = left_basis.reshape(flat_q), left_gram.reshape(flat_q)
    wide = pltpu.VMEM((N_SHARD * MSG, 128), F32)
    mats = pltpu.VMEM((N_SHARD * QMSG, 128), F32)
    full = pltpu.VMEM((2, D, D), F32)
    half = pltpu.VMEM((2, D, D), BF16)
    hats = pltpu.VMEM((CAP, D, 128), F32)
    back_d, back_n, basis, gram = pl.pallas_call(
        main_kernel,
        out_shape=(
            jax.ShapeDtypeStruct((N_SHARD * MSG, 128), F32),
            jax.ShapeDtypeStruct((N_SHARD * MSG, 128), F32),
            jax.ShapeDtypeStruct((2, D, 96), F32),
            jax.ShapeDtypeStruct((2, D, 96), F32),
        ),
        in_specs=[smem] + [anyw] * 5,
        out_specs=(vmem,) * 4,
        scratch_shapes=[pltpu.VMEM(flat, F32)] * 3
        + [pltpu.VMEM(flat_q, F32)] * 2
        + [pltpu.VMEM((ZERO_CHUNK + 1, ROWS, 128), F32), pltpu.VMEM((ZERO_MAT + 1, ROWS, 128), F32)]
        + [wide] * 3
        + [mats] * 2
        + [wide] * 3
        + [mats]
        + [pltpu.VMEM((N_TENSOR, N_SHARD * QMSG, 128), F32)]
        + [wide] * 2
        + [full, pltpu.VMEM((N_TENSOR, 2, 96, D), F32), full]
        + [half] * 4
        + [hats] * 2
        + [
            pltpu.SemaphoreType.DMA((5,)),
            pltpu.SemaphoreType.DMA((10,)),
            pltpu.SemaphoreType.DMA((10,)),
            pltpu.SemaphoreType.DMA((10,)),
        ],
        compiler_params=pltpu.CompilerParams(
            collective_id=0, has_side_effects=True, vmem_limit_bytes=48 << 20
        ),
        name="exchange_and_rotate",
    )(tab, g, m, v, q, s)
    weight_new, first_new, second_new = pl.pallas_call(
        unpack_kernel,
        out_shape=(jax.ShapeDtypeStruct(flat, F32),) * 3,
        in_specs=[smem] + [vmem] * 5,
        out_specs=(vmem,) * 3,
        name="unpack",
    )(tab, back_d, back_n, w, g, m)
    bias_first_new = 0.9 * bias_first + 0.1 * bias_gradient
    bias_second_new = 0.95 * bias_second + 0.05 * bias_gradient * bias_gradient
    bias_updated = bias_weight - 0.01 * adam_direction(bias_first_new, bias_second_new)
    return (
        weight_new.reshape(weight.shape),
        first_new.reshape(weight.shape),
        second_new.reshape(weight.shape),
        basis[None],
        gram[None],
        bias_updated,
        bias_first_new,
        bias_second_new,
    )


def solution(mesh):
    rows = P("shard", "tensor", None)
    flat = P(("shard", "tensor"))
    owned = P("shard", None, None, "tensor")
    return jax.shard_map(
        body,
        mesh=mesh,
        in_specs=(rows,) * 6 + (P(),) + (flat,) * 4,
        out_specs=(rows,) * 3 + (owned,) * 2 + (flat,) * 3,
        check_vma=False,
    )
```

profile of v0, /device:TPU:1, one launch (start us, length us, event | category | flops | bytes accessed | tf_op | source)
XLA Modules:
  0.0 111.9 jit_solution(10062301510446713066)
XLA Ops:
  0.6 0.0 copy-start.5
  0.6 1.4 %copy.25.owner_ref = s32[12,5]{1,0:T(8,128)} copy(s32[12,5]{0,1:T(8,128)} %param.17) | data formatting | bytes 480 | tf_op args[6]
  2.1 4.3 %tables.1.tab = s32[512]{0:T(512)} custom-call(s32[12,5]{1,0:T(8,128)} %copy.25.owner_ref), custom_call_target="tpu_custom_call" | custom-call | tf_op jit(solution)/shard_map/tables/pallas_call | solution.py:476
  6.4 1.4 %multiply_subtract_fusion = (f32[540]{0:T(1024)}, f32[540]{0:T(1024)}, f32[540]{0:T(1024)}) fusion(f32[540]{0:T(1024)} %param.19, f32[540]{0:T(1024)} %param.18, f32[540]{0:T(1024)} %param.20, f32[540]{0:T(1024)} %param.21), kind=kLoop, calls=%fused_computation.2 | loop fusion | flops 7020 | bytes 15120 | tf_op jit(solution)/shard_map/sub | solution.py:534
  7.7 0.0 copy-start
  7.7 0.0 copy-start.1
  7.7 0.0 copy-start.4
  7.7 1.8 %reduce = f32[12,5760]{1,0:T(8,128)S(1)} reduce(f32[12,1,5760]{2,1,0:T(1,128)} %param.15, f32[]{:T(128)} %constant.28), dimensions={1}, to_apply=%param.15.reduce_sub_computation | reduce | bytes 552964 | tf_op args[4]
  9.5 0.0 copy-done.5
  9.5 0.7 reduce.1
  10.3 0.0 copy-done
  10.3 0.0 copy-done.1
  10.3 0.0 copy-done.4
  10.3 0.0 copy-start.3
  10.3 1.2 %copy-done.3 = f32[12,1,20736]{2,1,0:T(1,128)S(1)} copy-done((f32[12,1,20736]{2,1,0:T(1,128)S(1)}, f32[12,1,20736]{2,1,0:T(1,128)}, u32[]{:S(2)}) %copy-start.3) | copy-done | bytes 995352
  11.5 92.3 %exchange_and_rotate.1 = (f32[2304,128]{1,0:T(8,128)S(1)}, f32[2304,128]{1,0:T(8,128)}, f32[2,384,96]{2,1,0:T(8,128)S(1)}, f32[2,384,96]{2,1,0:T(8,128)S(1)}) custom-call(s32[512]{0:T(512)S(1)} %copy-done.4, f32[1944,128]{1,0:T(8,128)S(1)} %bitcast.10, f32[1944,128]{1,0:T(8,128)S(1)} %bitcast.12, f32[1944,128]{1,0:T(8,128)S(1)} %bitcast.13, ...), custom_call_target="tpu_custom_call" | custom-call | tf_op jit(solution)/shard_map/exchange_and_rotate/pallas_call | solution.py:492
  103.8 0.0 copy-start.2
  103.8 1.0 copy-done.2
  104.8 0.9 copy.29
  105.7 0.9 copy.30
  106.6 5.4 %unpack.1 = (f32[1944,128]{1,0:T(8,128)}, f32[1944,128]{1,0:T(8,128)}, f32[1944,128]{1,0:T(8,128)}) custom-call(s32[512]{0:T(512)} %tables.1.tab, f32[2304,128]{1,0:T(8,128)} %copy-done.2, f32[2304,128]{1,0:T(8,128)} %get-tuple-element.16.back_n, f32[1944,128]{1,0:T(8,128)} %bitcast.16, f32[1944,128]{1,0:T(8,128)} %bitcast.9, f32[1944,128]{1,0:T(8,128)} %bitcast.11), custom_call_target="tpu_custom_call" | custom-call | tf_op jit(solution)/shard_map/unpack/pallas_call | solution.py:525
  (2 shorter events, 0.1 us)
Async XLA Ops:
  0.6 8.9 %copy-start.5 = (f32[12,1,5760]{2,1,0:T(1,128)S(1)}, f32[12,1,5760]{2,1,0:T(1,128)}, u32[]{:S(2)}) copy-start(f32[12,1,5760]{2,1,0:T(1,128)} %param.16) | copy-start | bytes 829444
  7.7 2.6 %copy-start = (f32[12,1,20736]{2,1,0:T(1,128)S(1)}, f32[12,1,20736]{2,1,0:T(1,128)}, u32[]{:S(2)}) copy-start(f32[12,1,20736]{2,1,0:T(1,128)} %param.11) | copy-start | bytes 2985988
  7.7 2.6 %copy-start.1 = (f32[12,1,20736]{2,1,0:T(1,128)S(1)}, f32[12,1,20736]{2,1,0:T(1,128)}, u32[]{:S(2)}) copy-start(f32[12,1,20736]{2,1,0:T(1,128)} %param.13) | copy-start | bytes 2985988
  7.7 2.6 %copy-start.4 = (s32[512]{0:T(512)S(1)}, s32[512]{0:T(512)}, u32[]{:S(2)}) copy-start(s32[512]{0:T(512)} %tables.1.tab) | copy-start | bytes 6148
  10.3 1.2 %copy-start.3 = (f32[12,1,20736]{2,1,0:T(1,128)S(1)}, f32[12,1,20736]{2,1,0:T(1,128)}, u32[]{:S(2)}) copy-start(f32[12,1,20736]{2,1,0:T(1,128)} %param.14) | copy-start | bytes 2985988
  103.8 1.0 copy-start.2
where the time goes:
time: 112 us
  Pallas kernels  102 us (91%)
  local copies, waits for them, and re-layouts  5.47 us (5%)
  other arithmetic  3.8 us (3%)
    pallas_call x1, Pallas kernels, body(): pl.pallas_call(main_kernel, out_shape=(jax.ShapeDtypeStruct((N_SHARD * MS...  92.3 us
    unnamed x15, local copies, waits for them, and re-layouts  5.4 us
    pallas_call x1, Pallas kernels, body(): pl.pallas_call(unpack_kernel, out_shape=(jax.ShapeDtypeStruct(flat, F32),...  5.37 us
    pallas_call x1, Pallas kernels, body(): pl.pallas_call(table_kernel, out_shape=jax.ShapeDtypeStruct((TAB_SIZE,),...  4.29 us
    unnamed x2, other arithmetic  2.45 us

commit v1 on v0

--- a/solution.py
+++ b/solution.py
@@ -28,41 +28,37 @@
 ZERO_MAT = 60
 CORR_ONE = 1.0 - 0.9**STEP
 CORR_TWO = 1.0 - 0.95**STEP
-TAB_M = 256
-TAB_LOC = 320
-TAB_C0 = 384
-TAB_SIZE = 512
+NO_CODE = ZERO_MAT + (ZERO_CHUNK << 8)
+HEAD = 48
+TAIL = 24
+VMEM_ALL = 67043328
 F32 = jnp.float32
 BF16 = jnp.bfloat16
 
 
-def table_kernel(owner_ref, tab_ref):
-    @pl.loop(0, 256)
-    def _(i):
-        tab_ref[i] = ZERO_CHUNK
-
-    @pl.loop(0, 64)
-    def _(i):
-        tab_ref[TAB_M + i] = ZERO_MAT
-
-    @pl.loop(0, 32)
-    def _(i):
-        tab_ref[TAB_C0 + i] = 0
-
-    @pl.loop(0, 12)
-    def _(layer):
-        for kind in range(5):
-            mat = layer * 5 + kind
-            owner = owner_ref[layer, kind]
-            first = tab_ref[TAB_M + 2 * owner] == ZERO_MAT
-            chunks = TYPE_CHUNKS[kind]
-            held = tab_ref[TAB_C0 + owner]
-            base = jnp.where(first, 0, held)
-            tab_ref[TAB_M + 2 * owner + jnp.where(first, 0, 1)] = mat
-            tab_ref[TAB_C0 + owner] = jnp.where(first, chunks, held)
-            tab_ref[TAB_LOC + mat] = MSG * owner + base
-            for j in range(chunks):
-                tab_ref[owner * 8 + base + j] = layer * 15 + CHUNK_START[kind] + j
+def code_of(mat):
+    layer, kind = divmod(mat, 5)
+    return mat + ((layer * 15 + CHUNK_START[kind]) << 8) + (TYPE_CHUNKS[kind] << 16)
+
+
+def fill_tables(owner, chunk_tab, mat_tab, first_tab):
+    @pl.loop(0, N_SHARD)
+    def _(d):
+        first = jnp.int32(NO_CODE)
+        second = jnp.int32(NO_CODE)
+        for mat in range(60):
+            back = 59 - mat
+            first = jnp.where(owner[back % 5, back // 5] == d, code_of(back), first)
+            second = jnp.where(owner[mat % 5, mat // 5] == d, code_of(mat), second)
+        second = jnp.where(second == first, NO_CODE, second)
+        c0, c1 = first >> 16, second >> 16
+        at0, at1 = (first >> 8) & 255, (second >> 8) & 255
+        mat_tab[2 * d] = first & 255
+        mat_tab[2 * d + 1] = second & 255
+        first_tab[d] = c0
+        for k in range(CAP):
+            rest = jnp.where(k - c0 < c1, at1 + k - c0, ZERO_CHUNK)
+            chunk_tab[8 * d + k] = jnp.where(k < c0, at0 + k, rest)
 
 
 def align_rows(src, dst):
@@ -95,11 +91,11 @@
     def _(quad):
         for part in range(4):
             at, shift = divmod(96 * part, 128)
-            val = src[pl.ds(3 * quad + at, ROWS, stride=QLINE), :]
+            val = src[3 * quad + at]
             if shift:
                 val = pltpu.roll(val, 128 - shift, 1)
                 if 96 > 128 - shift:
-                    nxt = src[pl.ds(3 * quad + at + 1, ROWS, stride=QLINE), :]
+                    nxt = src[3 * quad + at + 1]
                     nxt = pltpu.roll(nxt, 128 - shift, 1)
                     val = jnp.where(lane < 128 - shift, val, nxt)
             dst[4 * quad + part] = jnp.where(lane < 96, val, 0.0)
@@ -124,7 +120,7 @@
 
 
 def main_kernel(
-    tab,
+    owner,
     g_hbm,
     m_hbm,
     v_hbm,
@@ -132,8 +128,10 @@
     s_hbm,
     back_d,
     back_n,
+    first_out,
     basis_out,
     gram_out,
+    loc_out,
     g2,
     m2,
     v2,
@@ -162,7 +160,14 @@
     qt_lo,
     g_hat,
     m_hat,
+    gram_strip,
+    basis_strip,
+    chunk_tab,
+    mat_tab,
+    first_tab,
     in_sem,
+    q_sem,
+    s_sem,
     send_sem,
     recv_sem,
     own_sem,
@@ -171,13 +176,23 @@
     rank = lax.axis_index("tensor")
     my_y, my_z, my_c = me // 8, (me // 2) % 4, me % 2
 
+    def chunk_load(src, dst, sem, c):
+        lanes = pl.ds(pl.multiple_of(128 * c, 128), 128)
+        return pltpu.make_async_copy(src.at[:, 0, lanes], dst.at[c], sem.at[c])
+
+    @pl.loop(0, QLINE)
+    def _(c):
+        chunk_load(q_hbm, q2, q_sem, c).start()
+
     loads = []
-    for n, (src, dst) in enumerate(
-        ((q_hbm, q2), (g_hbm, g2), (s_hbm, s2), (m_hbm, m2), (v_hbm, v2))
-    ):
+    for n, (src, dst) in enumerate(((g_hbm, g2), (m_hbm, m2), (v_hbm, v2))):
         load = pltpu.make_async_copy(src, dst, in_sem.at[n])
         load.start()
         loads.append(load)
+
+    @pl.loop(0, QLINE)
+    def _(c):
+        chunk_load(s_hbm, s2, s_sem, c).start()
 
     def peer(t):
         o = (11 * t) % 32
@@ -198,27 +213,31 @@
 
     lined[ZERO_CHUNK] = jnp.zeros((ROWS, 128), F32)
     lined_q[ZERO_MAT] = jnp.zeros((ROWS, 128), F32)
-
-    def exchange(send, recv, rows, n):
-        def one(t):
+    fill_tables(owner, chunk_tab, mat_tab, first_tab)
+
+    def own_copy(send, recv, unit, off, rows, n):
+        own = pl.ds(pl.multiple_of(me * unit + off, 8), rows)
+        return pltpu.make_async_copy(send.at[own], recv.at[own], own_sem.at[n])
+
+    def exchange(send, recv, unit, n, off=0, rows=None):
+        rows = unit if rows is None else rows
+
+        @pl.loop(1, N_SHARD)
+        def _(t):
             dst = peer(t)
-            return pltpu.make_async_remote_copy(
-                src_ref=send.at[pl.ds(pl.multiple_of(dst * rows, 8), rows)],
-                dst_ref=recv.at[pl.ds(pl.multiple_of(me * rows, 8), rows)],
+            pltpu.make_async_remote_copy(
+                src_ref=send.at[pl.ds(pl.multiple_of(dst * unit + off, 8), rows)],
+                dst_ref=recv.at[pl.ds(pl.multiple_of(me * unit + off, 8), rows)],
                 send_sem=send_sem.at[n],
                 recv_sem=recv_sem.at[n],
                 device_id=(dst, rank),
                 device_id_type=MESH,
-            )
-
-        @pl.loop(1, N_SHARD)
-        def _(t):
-            one(t).start()
-
-        own = pl.ds(pl.multiple_of(me * rows, 8), rows)
-        pltpu.make_async_copy(send.at[own], recv.at[own], own_sem.at[n]).start()
-
-    def exchange_done(send, recv, rows, n):
+            ).start()
+
+        own_copy(send, recv, unit, off, rows, n).start()
+
+    def exchange_done(send, recv, unit, n, off=0, rows=None):
+        rows = unit if rows is None else rows
         whole = pl.ds(0, (N_SHARD - 1) * rows)
         every = pltpu.make_async_remote_copy(
             src_ref=send.at[whole],
@@ -228,8 +247,7 @@
             device_id=((me + 1) % N_SHARD, rank),
             device_id_type=MESH,
         )
-        own = pl.ds(pl.multiple_of(me * rows, 8), rows)
-        pltpu.make_async_copy(send.at[own], recv.at[own], own_sem.at[n]).wait()
+        own_copy(send, recv, unit, off, rows, n).wait()
         every.wait_send()
         every.wait_recv()
 
@@ -237,40 +255,57 @@
         @pl.loop(0, N_SHARD)
         def _(d):
             for k in range(CAP):
-                send[pl.ds(MSG * d + k, ROWS, stride=CAP), :] = lines[tab[d * 8 + k]]
+                send[pl.ds(MSG * d + k, ROWS, stride=CAP), :] = lines[chunk_tab[d * 8 + k]]
 
     def pack_mats(lines, send):
         @pl.loop(0, N_SHARD)
         def _(d):
             for j in range(2):
-                send[pl.ds(QMSG * d + j, ROWS, stride=2), :] = lines[tab[TAB_M + 2 * d + j]]
-
-    loads[0].wait()
+                send[pl.ds(QMSG * d + j, ROWS, stride=2), :] = lines[mat_tab[2 * d + j]]
+
+    @pl.loop(0, QLINE)
+    def _(c):
+        chunk_load(q_hbm, q2, q_sem, c).wait()
+
     align_mats(q2, lined_q)
     pack_mats(lined_q, send_q)
     pl.semaphore_wait(barrier, N_SHARD - 1 + N_TENSOR - 1)
     exchange(send_q, qx.at[rank], QMSG, 0)
 
-    loads[1].wait()
+    loads[0].wait()
     align_rows(g2, lined)
     pack(lined, send_g)
     exchange(send_g, recv_g, MSG, 1)
 
-    loads[2].wait()
+    @pl.loop(0, QLINE)
+    def _(c):
+        chunk_load(s_hbm, s2, s_sem, c).wait()
+
     align_mats(s2, lined_q)
     pack_mats(lined_q, send_s)
     exchange(send_s, recv_s, QMSG, 2)
 
-    loads[3].wait()
+    loads[1].wait()
     m2[...] = 0.9 * m2[...] + 0.1 * g2[...]
+    save_first = pltpu.make_async_copy(m2, first_out, in_sem.at[3])
+    save_first.start()
     align_rows(m2, lined)
     pack(lined, send_m)
     exchange(send_m, recv_m, MSG, 3)
 
-    loads[4].wait()
+    loads[2].wait()
     align_rows(v2, lined)
     pack(lined, send_v)
-    exchange(send_v, recv_v, MSG, 4)
+    exchange(send_v, recv_v, MSG, 4, 0, HEAD)
+    exchange(send_v, recv_v, MSG, 10, HEAD, TAIL)
+
+    @pl.loop(0, 12)
+    def _(layer):
+        for kind in range(5):
+            mat = 5 * layer + kind
+            group = owner[kind, layer]
+            base = jnp.where(mat_tab[2 * group] == mat, 0, first_tab[group])
+            loc_out[mat] = MSG * group + base
 
     def spread(src_of, dst_of, n):
         for dx in range(1, N_TENSOR):
@@ -301,7 +336,7 @@
     spread(*q_part, 5)
 
     exchange_done(send_g, recv_g, MSG, 1)
-    c0 = tab[TAB_C0 + me]
+    c0 = first_tab[me]
     for j in range(2):
         left_h, left_l, right_h, right_l = [], [], [], []
         for k in range(CAP):
@@ -347,8 +382,8 @@
             [recv_g[pl.ds(k, D, stride=CAP), :], recv_m[pl.ds(k, D, stride=CAP), :]], axis=1
         )
         hat = dot3((qt_hi[sel], qt_lo[sel]), split(both), NN)
-        g_hat[k] = hat[:, :128]
-        m_hat[k] = hat[:, 128:]
+        g_hat[pl.ds(k, D, stride=CAP), :] = hat[:, :128]
+        m_hat[pl.ds(k, D, stride=CAP), :] = hat[:, 128:]
 
     spread_done(xg.at[pl.ds(0, 3)], 6)
     for j in range(2):
@@ -357,7 +392,7 @@
             total = total + xg[(rank + dx) % N_TENSOR, j]
         held = recv_s[pl.ds(j, D, stride=2), :].T[:96]
         fresh = 0.95 * held + 0.05 * total
-        gram_out[j] = fresh.T
+        gram_strip[j] = fresh
         power[j, strip(rank), :] = dot3(split(fresh), (q_hi[j], q_lo[j]), NN)
     p_part = (
         (lambda other: power.at[:, strip(rank), :]),
@@ -365,21 +400,26 @@
     )
     spread(*p_part, 7)
 
-    exchange_done(send_v, recv_v, MSG, 4)
-
-    @pl.loop(0, CAP)
-    def _(k):
-        rot = g_hat[k]
-        second = 0.95 * recv_v[pl.ds(k, D, stride=CAP), :] + 0.05 * rot * rot
-        ret_n[pl.ds(k, D, stride=CAP), :] = second
-        m_hat[k] = m_hat[k] / CORR_ONE / (jnp.sqrt(second / CORR_TWO) + 1e-08)
-
-    exchange(ret_n, back_n, MSG, 8)
+    for n, off, rows in ((4, 0, HEAD), (10, HEAD, TAIL)):
+        exchange_done(send_v, recv_v, MSG, n, off, rows)
+
+        @pl.loop(0, N_SHARD)
+        def _(s):
+            here = pl.ds(pl.multiple_of(MSG * s + off, 8), rows)
+            rot = g_hat[here, :]
+            ret_n[here, :] = 0.95 * recv_v[here, :] + 0.05 * rot * rot
+
+        exchange(ret_n, back_n, MSG, 8 if off == 0 else 11, off, rows)
+
+    @pl.loop(0, N_SHARD)
+    def _(s):
+        here = pl.ds(pl.multiple_of(MSG * s, 8), MSG)
+        m_hat[here, :] = m_hat[here, :] / CORR_ONE / (jnp.sqrt(ret_n[here, :] / CORR_TWO) + 1e-08)
 
     @pl.loop(0, CAP)
     def _(k):
         sel = jnp.where(k >= c0, 1, 0)
-        ret_d[pl.ds(k, D, stride=CAP), :] = dot3((q_hi[sel], q_lo[sel]), split(m_hat[k]), NN)
+        ret_d[pl.ds(k, D, stride=CAP), :] = dot3((q_hi[sel], q_lo[sel]), split(m_hat[pl.ds(k, D, stride=CAP), :]), NN)
 
     exchange(ret_d, back_d, MSG, 9)
 
@@ -401,10 +441,19 @@
 
         @pl.when(rank == x)
         def _():
-            basis_out[...] = power[:, :, 96 * x : 96 * x + 96]
-
-    exchange_done(ret_n, back_n, MSG, 8)
+            for j in range(2):
+                basis_strip[j] = power[j, :, 96 * x : 96 * x + 96].T
+
+    save_basis = pltpu.make_async_copy(basis_strip, basis_out, in_sem.at[4])
+    save_basis.start()
+    save_gram = pltpu.make_async_copy(gram_strip, gram_out, in_sem.at[5])
+    save_gram.start()
+    exchange_done(ret_n, back_n, MSG, 8, 0, HEAD)
+    exchange_done(ret_n, back_n, MSG, 11, HEAD, TAIL)
     exchange_done(ret_d, back_d, MSG, 9)
+    save_first.wait()
+    save_basis.wait()
+    save_gram.wait()
 
 
 def out_pieces():
@@ -430,31 +479,93 @@
     return table
 
 
-def unpack_kernel(tab, back_d, back_n, w2, g2, m2, weight_out, first_out, second_out):
+def unpack_kernel(
+    loc,
+    back_d,
+    back_n,
+    w_hbm,
+    first,
+    basis,
+    gram,
+    bias_g,
+    bias_w,
+    bias_m,
+    bias_v,
+    weight_out,
+    first_out,
+    second_out,
+    basis_out,
+    gram_out,
+    bias_w_out,
+    bias_m_out,
+    bias_v_out,
+    dv,
+    nv,
+    w2,
+    f2,
+    b2,
+    s2,
+    second2,
+    sem,
+    sem_out,
+):
+    def copy(src, dst, n, sems=sem):
+        made = pltpu.make_async_copy(src, dst, sems.at[n])
+        made.start()
+        return made
+
+    load_n = copy(back_n, nv, 0)
+    load_d = copy(back_d, dv, 1)
+    load_w = copy(w_hbm, w2, 2)
+    load_f = copy(first, f2, 3)
+    load_b = copy(basis, b2, 4)
+    load_s = copy(gram, s2, 5)
+
+    moment = 0.9 * bias_m[...] + 0.1 * bias_g[...]
+    second = 0.95 * bias_v[...] + 0.05 * bias_g[...] * bias_g[...]
+    bias_m_out[...] = moment
+    bias_v_out[...] = second
+    bias_w_out[...] = bias_w[...] - 0.01 * (
+        moment / CORR_ONE / (jnp.sqrt(second / CORR_TWO) + 1e-08)
+    )
     lane = lax.broadcasted_iota(jnp.int32, (ROWS, 128), 1)
     table = out_pieces()
 
-    @pl.loop(0, PAIRS)
-    def _(pair):
-        for chunk in range(27):
-            vals = [None, None]
-            for (mat, j, turn), _lo, hi in reversed(table[chunk]):
-                at = tab[TAB_LOC + 10 * pair + mat] + j
-                for n, back in enumerate((back_d, back_n)):
+    def unpack(back, write):
+        @pl.loop(0, PAIRS)
+        def _(pair):
+            for chunk in range(27):
+                out = None
+                for (mat, j, turn), _lo, hi in reversed(table[chunk]):
+                    at = loc[10 * pair + mat] + j
                     val = back[pl.ds(at, ROWS, stride=CAP), :]
                     if turn:
                         val = pltpu.roll(val, turn, 1)
-                    vals[n] = val if vals[n] is None else jnp.where(lane < hi, val, vals[n])
-            here = pl.ds(27 * pair + chunk, ROWS, stride=LINE)
-            w = w2[here, :]
-            weight_out[here, :] = w - 0.01 * (vals[0] + 0.1 * w)
-            second_out[here, :] = vals[1]
-
-    first_out[...] = 0.9 * m2[...] + 0.1 * g2[...]
-
-
-def adam_direction(moment_hat, second_new):
-    return moment_hat / CORR_ONE / (jnp.sqrt(second_new / CORR_TWO) + 1e-08)
+                    out = val if out is None else jnp.where(lane < hi, val, out)
+                write(pl.ds(27 * pair + chunk, ROWS, stride=LINE), out)
+
+    def write_second(here, val):
+        second2[here, :] = val
+
+    def write_weight(here, val):
+        w = w2[here, :]
+        w2[here, :] = w - 0.01 * (val + 0.1 * w)
+
+    load_n.wait()
+    unpack(nv, write_second)
+    saves = [copy(second2, second_out, 0, sem_out)]
+    load_f.wait()
+    saves.append(copy(f2, first_out, 1, sem_out))
+    load_b.wait()
+    saves.append(copy(b2, basis_out, 2, sem_out))
+    load_s.wait()
+    saves.append(copy(s2, gram_out, 3, sem_out))
+    load_d.wait()
+    load_w.wait()
+    unpack(dv, write_weight)
+    saves.append(copy(w2, weight_out, 4, sem_out))
+    for save in saves:
+        save.wait()
 
 
 def body(
@@ -472,35 +583,33 @@
 ):
     smem = pl.BlockSpec(memory_space=pltpu.SMEM)
     vmem = pl.BlockSpec(memory_space=pltpu.VMEM)
-    anyw = pl.BlockSpec(memory_space=pl.ANY)
-    tab = pl.pallas_call(
-        table_kernel,
-        out_shape=jax.ShapeDtypeStruct((TAB_SIZE,), jnp.int32),
-        in_specs=[smem],
-        out_specs=smem,
-        name="tables",
-    )(owner_table)
+    hbm = pl.BlockSpec(memory_space=pltpu.HBM)
     flat = (ROWS * LINE, 128)
-    flat_q = (ROWS * QLINE, 128)
     g, w, m, v = (a.reshape(flat) for a in (gradient, weight, first_moment, second_moment))
-    q, s = left_basis.reshape(flat_q), left_gram.reshape(flat_q)
     wide = pltpu.VMEM((N_SHARD * MSG, 128), F32)
     mats = pltpu.VMEM((N_SHARD * QMSG, 128), F32)
     full = pltpu.VMEM((2, D, D), F32)
     half = pltpu.VMEM((2, D, D), BF16)
-    hats = pltpu.VMEM((CAP, D, 128), F32)
-    back_d, back_n, basis, gram = pl.pallas_call(
+    strips = pltpu.VMEM((2, 96, D), F32)
+    rows = pltpu.VMEM(flat, F32)
+    lines_q = pltpu.VMEM((QLINE, ROWS, 128), F32)
+    wide_out = jax.ShapeDtypeStruct((N_SHARD * MSG, 128), F32)
+    flat_out = jax.ShapeDtypeStruct(flat, F32)
+    strip_out = jax.ShapeDtypeStruct((2, 96, D), F32)
+    back_d, back_n, first, basis, gram, loc = pl.pallas_call(
         main_kernel,
         out_shape=(
-            jax.ShapeDtypeStruct((N_SHARD * MSG, 128), F32),
-            jax.ShapeDtypeStruct((N_SHARD * MSG, 128), F32),
-            jax.ShapeDtypeStruct((2, D, 96), F32),
-            jax.ShapeDtypeStruct((2, D, 96), F32),
+            wide_out,
+            wide_out,
+            flat_out,
+            strip_out,
+            strip_out,
+            jax.ShapeDtypeStruct((64,), jnp.int32),
         ),
-        in_specs=[smem] + [anyw] * 5,
-        out_specs=(vmem,) * 4,
-        scratch_shapes=[pltpu.VMEM(flat, F32)] * 3
-        + [pltpu.VMEM(flat_q, F32)] * 2
+        in_specs=[smem] + [hbm] * 5,
+        out_specs=(hbm,) * 5 + (smem,),
+        scratch_shapes=[rows] * 3
+        + [lines_q] * 2
         + [pltpu.VMEM((ZERO_CHUNK + 1, ROWS, 128), F32), pltpu.VMEM((ZERO_MAT + 1, ROWS, 128), F32)]
         + [wide] * 3
         + [mats] * 2
@@ -510,37 +619,58 @@
         + [wide] * 2
         + [full, pltpu.VMEM((N_TENSOR, 2, 96, D), F32), full]
         + [half] * 4
-        + [hats] * 2
+        + [wide] * 2
+        + [strips] * 2
         + [
-            pltpu.SemaphoreType.DMA((5,)),
-            pltpu.SemaphoreType.DMA((10,)),
-            pltpu.SemaphoreType.DMA((10,)),
-            pltpu.SemaphoreType.DMA((10,)),
+            pltpu.SMEM((256,), jnp.int32),
+            pltpu.SMEM((64,), jnp.int32),
+            pltpu.SMEM((32,), jnp.int32),
+            pltpu.SemaphoreType.DMA((6,)),
+            pltpu.SemaphoreType.DMA((QLINE,)),
+            pltpu.SemaphoreType.DMA((QLINE,)),
+            pltpu.SemaphoreType.DMA((12,)),
+            pltpu.SemaphoreType.DMA((12,)),
+            pltpu.SemaphoreType.DMA((12,)),
         ],
         compiler_params=pltpu.CompilerParams(
-            collective_id=0, has_side_effects=True, vmem_limit_bytes=48 << 20
+            collective_id=0, has_side_effects=True, vmem_limit_bytes=VMEM_ALL
         ),
         name="exchange_and_rotate",
-    )(tab, g, m, v, q, s)
-    weight_new, first_new, second_new = pl.pallas_call(
+    )(owner_table.T, g, m, v, left_basis, left_gram)
+    bias_out = jax.ShapeDtypeStruct(bias_gradient.shape, F32)
+    outs = pl.pallas_call(
         unpack_kernel,
-        out_shape=(jax.ShapeDtypeStruct(flat, F32),) * 3,
-        in_specs=[smem] + [vmem] * 5,
-        out_specs=(vmem,) * 3,
+        out_shape=(flat_out,) * 3 + (strip_out,) * 2 + (bias_out,) * 3,
+        in_specs=[smem] + [hbm] * 6 + [vmem] * 4,
+        out_specs=(hbm,) * 5 + (vmem,) * 3,
+        scratch_shapes=[wide] * 2
+        + [rows] * 2
+        + [strips] * 2
+        + [rows]
+        + [pltpu.SemaphoreType.DMA((6,)), pltpu.SemaphoreType.DMA((5,))],
+        compiler_params=pltpu.CompilerParams(vmem_limit_bytes=VMEM_ALL),
         name="unpack",
-    )(tab, back_d, back_n, w, g, m)
-    bias_first_new = 0.9 * bias_first + 0.1 * bias_gradient
-    bias_second_new = 0.95 * bias_second + 0.05 * bias_gradient * bias_gradient
-    bias_updated = bias_weight - 0.01 * adam_direction(bias_first_new, bias_second_new)
+    )(
+        loc,
+        back_d,
+        back_n,
+        w,
+        first,
+        basis,
+        gram,
+        bias_gradient,
+        bias_weight,
+        bias_first,
+        bias_second,
+    )
+    weight_new, first_new, second_new, basis_new, gram_new = outs[:5]
     return (
         weight_new.reshape(weight.shape),
         first_new.reshape(weight.shape),
         second_new.reshape(weight.shape),
-        basis[None],
-        gram[None],
-        bias_updated,
-        bias_first_new,
-        bias_second_new,
+        basis_new.transpose(0, 2, 1)[None],
+        gram_new.transpose(0, 2, 1)[None],
+        *outs[5:],
     )
 
 

time: 112 us -> 96.4 us (0.86)
  Pallas kernels: 102 us -> 95.6 us
  local copies, waits for them, and re-layouts: 5.47 us -> 0 us
  other arithmetic: 3.8 us -> 0 us
    pallas_call x3 -> x2, Pallas kernels: 102 us -> 95.6 us  [the longest x1 89.9 us: body(): pl.pallas_call(main_kernel, out_shape=(wide_out, wide_out, flat_out, stri...]
    unnamed x15 -> x0, local copies, waits for them, and re-layouts: 5.4 us -> none
    unnamed x2 -> x0, other arithmetic: 2.45 us -> none
    sub x1 -> x0, other arithmetic: 1.36 us -> none  [body(): bias_weight - 0.01 * adam_direction(bias_first_new, bias_second_new)]
where the time goes in v1:
time: 96.4 us; the launch traced here: 96.3 us
  Pallas kernels  95.6 us (99%)
    pallas_call x1, Pallas kernels, body(): pl.pallas_call(main_kernel, out_shape=(wide_out, wide_out, flat_out, stri...  89.9 us
    pallas_call x1, Pallas kernels, body(): pl.pallas_call(unpack_kernel, out_shape=(flat_out,) * 3 + (strip_out,) *...  5.71 us

profile of v1, /device:TPU:1, one launch (start us, length us, event | category | flops | bytes accessed | tf_op | source)
XLA Modules:
  0.0 96.3 jit_solution(11156091753853757744)
XLA Ops:
  0.6 89.9 %exchange_and_rotate.1 = (f32[2304,128]{1,0:T(8,128)}, f32[2304,128]{1,0:T(8,128)}, f32[1944,128]{1,0:T(8,128)}, f32[2,96,384]{2,1,0:T(8,128)}, f32[2,96,384]{2,1,0:T(8,128)}, /*index=5*/s32[64]{0:T(128)}) custom-call(s32[5,12]{1,0:T(8,128)} %bitcast.18, f32[1944,128]{1,0:T(8,128)} %bitcast.15, f32[1944,128]{1,0:T(8,128)} %bitcast.16, f32[1944,128]{1,0:T(8,128)} %bitcast.17, ...), custom_call_target="tpu_custom_call" | custom-call | tf_op jit(solution)/shard_map/exchange_and_rotate/pallas_call | solution.py:599
  90.5 5.7 %unpack.1 = (f32[1944,128]{1,0:T(8,128)}, f32[1944,128]{1,0:T(8,128)}, f32[1944,128]{1,0:T(8,128)}, f32[2,96,384]{2,1,0:T(8,128)}, f32[2,96,384]{2,1,0:T(8,128)}...) custom-call(s32[64]{0:T(128)} %get-tuple-element.22.loc, f32[2304,128]{1,0:T(8,128)} %get-tuple-element.23.back_d, ...), custom_call_target="tpu_custom_call" | custom-call | tf_op jit(solution)/shard_map/unpack/pallas_call | solution.py:641

commit v2 on v1

--- a/solution.py
+++ b/solution.py
@@ -28,7 +28,7 @@
 ZERO_MAT = 60
 CORR_ONE = 1.0 - 0.9**STEP
 CORR_TWO = 1.0 - 0.95**STEP
-NO_CODE = ZERO_MAT + (ZERO_CHUNK << 8)
+NO_CODE = (ZERO_MAT << 16) + (ZERO_CHUNK << 8)
 HEAD = 48
 TAIL = 24
 VMEM_ALL = 67043328
@@ -36,29 +36,34 @@
 BF16 = jnp.bfloat16
 
 
-def code_of(mat):
-    layer, kind = divmod(mat, 5)
-    return mat + ((layer * 15 + CHUNK_START[kind]) << 8) + (TYPE_CHUNKS[kind] << 16)
-
-
-def fill_tables(owner, chunk_tab, mat_tab, first_tab):
-    @pl.loop(0, N_SHARD)
-    def _(d):
-        first = jnp.int32(NO_CODE)
-        second = jnp.int32(NO_CODE)
-        for mat in range(60):
-            back = 59 - mat
-            first = jnp.where(owner[back % 5, back // 5] == d, code_of(back), first)
-            second = jnp.where(owner[mat % 5, mat // 5] == d, code_of(mat), second)
-        second = jnp.where(second == first, NO_CODE, second)
-        c0, c1 = first >> 16, second >> 16
-        at0, at1 = (first >> 8) & 255, (second >> 8) & 255
-        mat_tab[2 * d] = first & 255
-        mat_tab[2 * d + 1] = second & 255
-        first_tab[d] = c0
-        for k in range(CAP):
-            rest = jnp.where(k - c0 < c1, at1 + k - c0, ZERO_CHUNK)
-            chunk_tab[8 * d + k] = jnp.where(k < c0, at0 + k, rest)
+def table_of(owners):
+    group = lax.broadcasted_iota(jnp.int32, (N_SHARD, 12), 0)
+    layer = lax.broadcasted_iota(jnp.int32, (N_SHARD, 12), 1)
+    low = jnp.full((N_SHARD, 12), NO_CODE, jnp.int32)
+    high = jnp.full((N_SHARD, 12), -1, jnp.int32)
+    for kind in range(5):
+        code = ((5 * layer + kind) << 16) + ((15 * layer + CHUNK_START[kind]) << 8)
+        code = code + TYPE_CHUNKS[kind]
+        hit = owners[kind : kind + 1, :] == group
+        low = jnp.minimum(low, jnp.where(hit, code, NO_CODE))
+        high = jnp.maximum(high, jnp.where(hit, code, -1))
+    first = jnp.min(low, axis=1, keepdims=True)
+    second = jnp.max(high, axis=1, keepdims=True)
+    second = jnp.where((second < 0) | (second == first), NO_CODE, second)
+    c0, c1 = first & 255, second & 255
+    at0, at1 = (first >> 8) & 255, (second >> 8) & 255
+    k = lax.broadcasted_iota(jnp.int32, (N_SHARD, 128), 1)
+    rest = jnp.where(k - c0 < c1, at1 + k - c0, ZERO_CHUNK)
+    table = jnp.where(k < c0, at0 + k, rest)
+    table = jnp.where(k == 8, first >> 16, table)
+    table = jnp.where(k == 9, second >> 16, table)
+    return jnp.where(k == 10, c0, table)
+
+
+def place_of(owner, tab, pair, mat):
+    group = owner[mat % 5, 2 * pair + mat // 5]
+    base = jnp.where(tab[group, 8] == 10 * pair + mat, 0, tab[group, 10])
+    return MSG * group + base
 
 
 def align_rows(src, dst):
@@ -91,11 +96,11 @@
     def _(quad):
         for part in range(4):
             at, shift = divmod(96 * part, 128)
-            val = src[3 * quad + at]
+            val = src[pl.ds(3 * quad + at, ROWS, stride=QLINE), :]
             if shift:
                 val = pltpu.roll(val, 128 - shift, 1)
                 if 96 > 128 - shift:
-                    nxt = src[3 * quad + at + 1]
+                    nxt = src[pl.ds(3 * quad + at + 1, ROWS, stride=QLINE), :]
                     nxt = pltpu.roll(nxt, 128 - shift, 1)
                     val = jnp.where(lane < 128 - shift, val, nxt)
             dst[4 * quad + part] = jnp.where(lane < 96, val, 0.0)
@@ -119,19 +124,60 @@
 NT = ((1,), (1,))
 
 
+def out_pieces():
+    owner_of = []
+    for half in range(2):
+        for kind in range(5):
+            start = 1728 * half + 96 * TYPE_START[kind]
+            for c in range(96 * TYPE_TILES[kind]):
+                owner_of.append((5 * half + kind, start))
+    table = []
+    for chunk in range(27):
+        pieces = []
+        for lane in range(128):
+            col = 128 * chunk + lane
+            mat, start = owner_of[col]
+            j, src = divmod(col - start, 128)
+            key = (mat, j, (lane - src) % 128)
+            if pieces and pieces[-1][0] == key:
+                pieces[-1][2] = lane + 1
+            else:
+                pieces.append([key, lane, lane + 1])
+        table.append(pieces)
+    return table
+
+
+def unpack(back, owner, tab, write):
+    lane = lax.broadcasted_iota(jnp.int32, (ROWS, 128), 1)
+    table = out_pieces()
+
+    @pl.loop(0, PAIRS)
+    def _(pair):
+        places = [place_of(owner, tab, pair, mat) for mat in range(10)]
+        for chunk in range(27):
+            out = None
+            for (mat, j, turn), _lo, hi in reversed(table[chunk]):
+                val = back[pl.ds(places[mat] + j, ROWS, stride=CAP), :]
+                if turn:
+                    val = pltpu.roll(val, turn, 1)
+                out = val if out is None else jnp.where(lane < hi, val, out)
+            write(pl.ds(27 * pair + chunk, ROWS, stride=LINE), out)
+
+
 def main_kernel(
     owner,
+    owners,
     g_hbm,
     m_hbm,
     v_hbm,
     q_hbm,
     s_hbm,
     back_d,
-    back_n,
+    second_out,
     first_out,
     basis_out,
     gram_out,
-    loc_out,
+    tab_out,
     g2,
     m2,
     v2,
@@ -162,12 +208,11 @@
     m_hat,
     gram_strip,
     basis_strip,
-    chunk_tab,
-    mat_tab,
-    first_tab,
+    back_n,
+    second2,
+    tab_vec,
+    tab,
     in_sem,
-    q_sem,
-    s_sem,
     send_sem,
     recv_sem,
     own_sem,
@@ -176,24 +221,6 @@
     rank = lax.axis_index("tensor")
     my_y, my_z, my_c = me // 8, (me // 2) % 4, me % 2
 
-    def chunk_load(src, dst, sem, c):
-        lanes = pl.ds(pl.multiple_of(128 * c, 128), 128)
-        return pltpu.make_async_copy(src.at[:, 0, lanes], dst.at[c], sem.at[c])
-
-    @pl.loop(0, QLINE)
-    def _(c):
-        chunk_load(q_hbm, q2, q_sem, c).start()
-
-    loads = []
-    for n, (src, dst) in enumerate(((g_hbm, g2), (m_hbm, m2), (v_hbm, v2))):
-        load = pltpu.make_async_copy(src, dst, in_sem.at[n])
-        load.start()
-        loads.append(load)
-
-    @pl.loop(0, QLINE)
-    def _(c):
-        chunk_load(s_hbm, s2, s_sem, c).start()
-
     def peer(t):
         o = (11 * t) % 32
         return (
@@ -211,9 +238,22 @@
             barrier, inc=1, device_id=(me, (rank + dx) % N_TENSOR), device_id_type=MESH
         )
 
+    def local(src, dst, n):
+        made = pltpu.make_async_copy(src, dst, in_sem.at[n])
+        made.start()
+        return made
+
+    load_q = local(q_hbm.at[:, 0, :], q2, 0)
+    load_g = local(g_hbm, g2, 1)
+    load_s = local(s_hbm.at[:, 0, :], s2, 2)
+    load_m = local(m_hbm, m2, 3)
+    load_v = local(v_hbm, v2, 4)
+    tab_vec[...] = table_of(owners[...])
+    load_tab = local(tab_vec, tab, 5)
+    save_tab = local(tab_vec, tab_out, 6)
+
     lined[ZERO_CHUNK] = jnp.zeros((ROWS, 128), F32)
     lined_q[ZERO_MAT] = jnp.zeros((ROWS, 128), F32)
-    fill_tables(owner, chunk_tab, mat_tab, first_tab)
 
     def own_copy(send, recv, unit, off, rows, n):
         own = pl.ds(pl.multiple_of(me * unit + off, 8), rows)
@@ -255,57 +295,41 @@
         @pl.loop(0, N_SHARD)
         def _(d):
             for k in range(CAP):
-                send[pl.ds(MSG * d + k, ROWS, stride=CAP), :] = lines[chunk_tab[d * 8 + k]]
+                send[pl.ds(MSG * d + k, ROWS, stride=CAP), :] = lines[tab[d, k]]
 
     def pack_mats(lines, send):
         @pl.loop(0, N_SHARD)
         def _(d):
             for j in range(2):
-                send[pl.ds(QMSG * d + j, ROWS, stride=2), :] = lines[mat_tab[2 * d + j]]
-
-    @pl.loop(0, QLINE)
-    def _(c):
-        chunk_load(q_hbm, q2, q_sem, c).wait()
-
+                send[pl.ds(QMSG * d + j, ROWS, stride=2), :] = lines[tab[d, 8 + j]]
+
+    load_q.wait()
     align_mats(q2, lined_q)
+    load_g.wait()
+    align_rows(g2, lined)
+    load_tab.wait()
     pack_mats(lined_q, send_q)
+    pack(lined, send_g)
+    load_s.wait()
+    align_mats(s2, lined_q)
+    pack_mats(lined_q, send_s)
     pl.semaphore_wait(barrier, N_SHARD - 1 + N_TENSOR - 1)
     exchange(send_q, qx.at[rank], QMSG, 0)
-
-    loads[0].wait()
-    align_rows(g2, lined)
-    pack(lined, send_g)
     exchange(send_g, recv_g, MSG, 1)
-
-    @pl.loop(0, QLINE)
-    def _(c):
-        chunk_load(s_hbm, s2, s_sem, c).wait()
-
-    align_mats(s2, lined_q)
-    pack_mats(lined_q, send_s)
     exchange(send_s, recv_s, QMSG, 2)
 
-    loads[1].wait()
+    load_m.wait()
     m2[...] = 0.9 * m2[...] + 0.1 * g2[...]
-    save_first = pltpu.make_async_copy(m2, first_out, in_sem.at[3])
-    save_first.start()
+    save_first = local(m2, first_out, 7)
     align_rows(m2, lined)
     pack(lined, send_m)
     exchange(send_m, recv_m, MSG, 3)
 
-    loads[2].wait()
+    load_v.wait()
     align_rows(v2, lined)
     pack(lined, send_v)
     exchange(send_v, recv_v, MSG, 4, 0, HEAD)
     exchange(send_v, recv_v, MSG, 10, HEAD, TAIL)
-
-    @pl.loop(0, 12)
-    def _(layer):
-        for kind in range(5):
-            mat = 5 * layer + kind
-            group = owner[kind, layer]
-            base = jnp.where(mat_tab[2 * group] == mat, 0, first_tab[group])
-            loc_out[mat] = MSG * group + base
 
     def spread(src_of, dst_of, n):
         for dx in range(1, N_TENSOR):
@@ -336,7 +360,7 @@
     spread(*q_part, 5)
 
     exchange_done(send_g, recv_g, MSG, 1)
-    c0 = first_tab[me]
+    c0 = tab[me, 10]
     for j in range(2):
         left_h, left_l, right_h, right_l = [], [], [], []
         for k in range(CAP):
@@ -444,46 +468,27 @@
             for j in range(2):
                 basis_strip[j] = power[j, :, 96 * x : 96 * x + 96].T
 
-    save_basis = pltpu.make_async_copy(basis_strip, basis_out, in_sem.at[4])
-    save_basis.start()
-    save_gram = pltpu.make_async_copy(gram_strip, gram_out, in_sem.at[5])
-    save_gram.start()
+    save_basis = local(basis_strip, basis_out, 8)
+    save_gram = local(gram_strip, gram_out, 9)
     exchange_done(ret_n, back_n, MSG, 8, 0, HEAD)
     exchange_done(ret_n, back_n, MSG, 11, HEAD, TAIL)
+
+    def write_second(here, val):
+        second2[here, :] = val
+
+    unpack(back_n, owner, tab, write_second)
+    save_second = local(second2, second_out, 10)
+    for save in (save_tab, save_first, save_basis, save_gram, save_second):
+        save.wait()
     exchange_done(ret_d, back_d, MSG, 9)
-    save_first.wait()
-    save_basis.wait()
-    save_gram.wait()
-
-
-def out_pieces():
-    owner_of = []
-    for half in range(2):
-        for kind in range(5):
-            start = 1728 * half + 96 * TYPE_START[kind]
-            for c in range(96 * TYPE_TILES[kind]):
-                owner_of.append((5 * half + kind, start))
-    table = []
-    for chunk in range(27):
-        pieces = []
-        for lane in range(128):
-            col = 128 * chunk + lane
-            mat, start = owner_of[col]
-            j, src = divmod(col - start, 128)
-            key = (mat, j, (lane - src) % 128)
-            if pieces and pieces[-1][0] == key:
-                pieces[-1][2] = lane + 1
-            else:
-                pieces.append([key, lane, lane + 1])
-        table.append(pieces)
-    return table
 
 
 def unpack_kernel(
-    loc,
+    owner,
+    tab,
     back_d,
-    back_n,
     w_hbm,
+    second,
     first,
     basis,
     gram,
@@ -500,12 +505,11 @@
     bias_m_out,
     bias_v_out,
     dv,
-    nv,
     w2,
+    n2,
     f2,
     b2,
     s2,
-    second2,
     sem,
     sem_out,
 ):
@@ -514,55 +518,38 @@
         made.start()
         return made
 
-    load_n = copy(back_n, nv, 0)
-    load_d = copy(back_d, dv, 1)
-    load_w = copy(w_hbm, w2, 2)
-    load_f = copy(first, f2, 3)
-    load_b = copy(basis, b2, 4)
-    load_s = copy(gram, s2, 5)
+    load_d = copy(back_d, dv, 0)
+    load_w = copy(w_hbm, w2, 1)
+    passed = []
+    for n, (src, held, dst) in enumerate(
+        (
+            (second, n2, second_out),
+            (first, f2, first_out),
+            (basis, b2, basis_out),
+            (gram, s2, gram_out),
+        )
+    ):
+        passed.append((copy(src, held, 2 + n), held, dst))
 
     moment = 0.9 * bias_m[...] + 0.1 * bias_g[...]
-    second = 0.95 * bias_v[...] + 0.05 * bias_g[...] * bias_g[...]
+    moment_two = 0.95 * bias_v[...] + 0.05 * bias_g[...] * bias_g[...]
     bias_m_out[...] = moment
-    bias_v_out[...] = second
+    bias_v_out[...] = moment_two
     bias_w_out[...] = bias_w[...] - 0.01 * (
-        moment / CORR_ONE / (jnp.sqrt(second / CORR_TWO) + 1e-08)
+        moment / CORR_ONE / (jnp.sqrt(moment_two / CORR_TWO) + 1e-08)
     )
-    lane = lax.broadcasted_iota(jnp.int32, (ROWS, 128), 1)
-    table = out_pieces()
-
-    def unpack(back, write):
-        @pl.loop(0, PAIRS)
-        def _(pair):
-            for chunk in range(27):
-                out = None
-                for (mat, j, turn), _lo, hi in reversed(table[chunk]):
-                    at = loc[10 * pair + mat] + j
-                    val = back[pl.ds(at, ROWS, stride=CAP), :]
-                    if turn:
-                        val = pltpu.roll(val, turn, 1)
-                    out = val if out is None else jnp.where(lane < hi, val, out)
-                write(pl.ds(27 * pair + chunk, ROWS, stride=LINE), out)
-
-    def write_second(here, val):
-        second2[here, :] = val
 
     def write_weight(here, val):
         w = w2[here, :]
         w2[here, :] = w - 0.01 * (val + 0.1 * w)
 
-    load_n.wait()
-    unpack(nv, write_second)
-    saves = [copy(second2, second_out, 0, sem_out)]
-    load_f.wait()
-    saves.append(copy(f2, first_out, 1, sem_out))
-    load_b.wait()
-    saves.append(copy(b2, basis_out, 2, sem_out))
-    load_s.wait()
-    saves.append(copy(s2, gram_out, 3, sem_out))
     load_d.wait()
     load_w.wait()
-    unpack(dv, write_weight)
+    saves = []
+    for n, (load, held, dst) in enumerate(passed):
+        load.wait()
+        saves.append(copy(held, dst, n, sem_out))
+    unpack(dv, owner, tab, write_weight)
     saves.append(copy(w2, weight_out, 4, sem_out))
     for save in saves:
         save.wait()
@@ -592,24 +579,27 @@
     half = pltpu.VMEM((2, D, D), BF16)
     strips = pltpu.VMEM((2, 96, D), F32)
     rows = pltpu.VMEM(flat, F32)
-    lines_q = pltpu.VMEM((QLINE, ROWS, 128), F32)
+    rows_q = pltpu.VMEM((ROWS * QLINE, 128), F32)
     wide_out = jax.ShapeDtypeStruct((N_SHARD * MSG, 128), F32)
     flat_out = jax.ShapeDtypeStruct(flat, F32)
     strip_out = jax.ShapeDtypeStruct((2, 96, D), F32)
-    back_d, back_n, first, basis, gram, loc = pl.pallas_call(
+    tab_shape = (N_SHARD, 128)
+    flat_q = (ROWS * QLINE, 1, 128)
+    owner = owner_table.T
+    back_d, second, first, basis, gram, tab = pl.pallas_call(
         main_kernel,
         out_shape=(
             wide_out,
-            wide_out,
+            flat_out,
             flat_out,
             strip_out,
             strip_out,
-            jax.ShapeDtypeStruct((64,), jnp.int32),
+            jax.ShapeDtypeStruct(tab_shape, jnp.int32),
         ),
-        in_specs=[smem] + [hbm] * 5,
-        out_specs=(hbm,) * 5 + (smem,),
+        in_specs=[smem, vmem] + [hbm] * 5,
+        out_specs=(hbm,) * 6,
         scratch_shapes=[rows] * 3
-        + [lines_q] * 2
+        + [rows_q] * 2
         + [pltpu.VMEM((ZERO_CHUNK + 1, ROWS, 128), F32), pltpu.VMEM((ZERO_MAT + 1, ROWS, 128), F32)]
         + [wide] * 3
         + [mats] * 2
@@ -621,40 +611,32 @@
         + [half] * 4
         + [wide] * 2
         + [strips] * 2
-        + [
-            pltpu.SMEM((256,), jnp.int32),
-            pltpu.SMEM((64,), jnp.int32),
-            pltpu.SMEM((32,), jnp.int32),
-            pltpu.SemaphoreType.DMA((6,)),
-            pltpu.SemaphoreType.DMA((QLINE,)),
-            pltpu.SemaphoreType.DMA((QLINE,)),
-            pltpu.SemaphoreType.DMA((12,)),
-            pltpu.SemaphoreType.DMA((12,)),
-            pltpu.SemaphoreType.DMA((12,)),
-        ],
+        + [wide, rows]
+        + [pltpu.VMEM(tab_shape, jnp.int32), pltpu.SMEM(tab_shape, jnp.int32)]
+        + [pltpu.SemaphoreType.DMA((n,)) for n in (11, 12, 12, 12)],
         compiler_params=pltpu.CompilerParams(
             collective_id=0, has_side_effects=True, vmem_limit_bytes=VMEM_ALL
         ),
         name="exchange_and_rotate",
-    )(owner_table.T, g, m, v, left_basis, left_gram)
+    )(owner, owner, g, m, v, left_basis.reshape(flat_q), left_gram.reshape(flat_q))
     bias_out = jax.ShapeDtypeStruct(bias_gradient.shape, F32)
     outs = pl.pallas_call(
         unpack_kernel,
         out_shape=(flat_out,) * 3 + (strip_out,) * 2 + (bias_out,) * 3,
-        in_specs=[smem] + [hbm] * 6 + [vmem] * 4,
+        in_specs=[smem] * 2 + [hbm] * 6 + [vmem] * 4,
         out_specs=(hbm,) * 5 + (vmem,) * 3,
-        scratch_shapes=[wide] * 2
-        + [rows] * 2
+        scratch_shapes=[wide]
+        + [rows] * 3
         + [strips] * 2
-        + [rows]
         + [pltpu.SemaphoreType.DMA((6,)), pltpu.SemaphoreType.DMA((5,))],
         compiler_params=pltpu.CompilerParams(vmem_limit_bytes=VMEM_ALL),
         name="unpack",
     )(
-        loc,
+        owner,
+        tab,
         back_d,
-        back_n,
         w,
+        second,
         first,
         basis,
         gram,

time: 96.4 us -> 94.4 us (0.979)
  Pallas kernels: 95.6 us -> 93.6 us
    pallas_call x1, Pallas kernels: 89.9 us -> 87.6 us  [body(): pl.pallas_call(main_kernel, out_shape=(wide_out, flat_out, flat_out, stri...]
where the time goes in v2:
time: 94.4 us; the launch traced here: 94.2 us
  Pallas kernels  93.6 us (99%)
    pallas_call x1, Pallas kernels, body(): pl.pallas_call(main_kernel, out_shape=(wide_out, flat_out, flat_out, stri...  87.6 us
    pallas_call x1, Pallas kernels, body(): pl.pallas_call(unpack_kernel, out_shape=(flat_out,) * 3 + (strip_out,) *...  5.98 us

profile of v2, /device:TPU:1, one launch (start us, length us, event | category | flops | bytes accessed | tf_op | source)
XLA Modules:
  0.0 94.2 jit_solution(15065576895668006910)
XLA Ops:
  0.6 87.6 %exchange_and_rotate.1 = (f32[2304,128]{1,0:T(8,128)}, f32[1944,128]{1,0:T(8,128)}, f32[1944,128]{1,0:T(8,128)}, f32[2,96,384]{2,1,0:T(8,128)}, f32[2,96,384]{2,1,0:T(8,128)}, /*index=5*/s32[32,128]{1,0:T(8,128)}) custom-call(s32[5,12]{1,0:T(8,128)} %bitcast.22, s32[5,12]{1,0:T(8,128)} %bitcast.23, f32[1944,128]{1,0:T(8,128)} %bitcast.16, ...), custom_call_target="tpu_custom_call" | custom-call | tf_op jit(solution)/shard_map/exchange_and_rotate/pallas_call | solution.py:589
  88.2 6.0 %unpack.1 = (f32[1944,128]{1,0:T(8,128)}, f32[1944,128]{1,0:T(8,128)}, f32[1944,128]{1,0:T(8,128)}, f32[2,96,384]{2,1,0:T(8,128)}, f32[2,96,384]{2,1,0:T(8,128)}...) custom-call(s32[5,12]{1,0:T(8,128)} %bitcast.24, s32[32,128]{1,0:T(8,128)} %get-tuple-element.22.tab, ...), custom_call_target="tpu_custom_call" | custom-call | tf_op jit(solution)/shard_map/unpack/pallas_call | solution.py:623

commit v3 on v2

--- a/solution.py
+++ b/solution.py
@@ -33,6 +33,21 @@
 TAIL = 24
 VMEM_ALL = 67043328
 F32 = jnp.float32
+
+
+def send_order():
+    rings = (
+        ((2, 2),),
+        ((1, 2), (2, 1), (3, 2), (2, 3)),
+        ((1, 1), (3, 3), (1, 3), (3, 1)),
+        ((2, 0), (0, 2)),
+        ((1, 0), (0, 1), (3, 0), (0, 3)),
+    )
+    order = [(dy, dz, dc) for ring in rings for dc in range(2) for dy, dz in ring]
+    return order + [(0, 0, 1)]
+
+
+ORDER = send_order()
 BF16 = jnp.bfloat16
 
 
@@ -92,18 +107,18 @@
 def align_mats(src, dst):
     lane = lax.broadcasted_iota(jnp.int32, (ROWS, 128), 1)
 
-    @pl.loop(0, 15)
-    def _(quad):
-        for part in range(4):
+    @pl.loop(0, 3)
+    def _(step):
+        for part in range(20):
             at, shift = divmod(96 * part, 128)
-            val = src[pl.ds(3 * quad + at, ROWS, stride=QLINE), :]
+            val = src[pl.ds(15 * step + at, ROWS, stride=QLINE), :]
             if shift:
                 val = pltpu.roll(val, 128 - shift, 1)
                 if 96 > 128 - shift:
-                    nxt = src[pl.ds(3 * quad + at + 1, ROWS, stride=QLINE), :]
+                    nxt = src[pl.ds(15 * step + at + 1, ROWS, stride=QLINE), :]
                     nxt = pltpu.roll(nxt, 128 - shift, 1)
                     val = jnp.where(lane < 128 - shift, val, nxt)
-            dst[4 * quad + part] = jnp.where(lane < 96, val, 0.0)
+            dst[20 * step + part] = jnp.where(lane < 96, val, 0.0)
 
 
 def split(x):
@@ -147,17 +162,16 @@
     return table
 
 
-def unpack(back, owner, tab, write):
+def unpack(back, place, write, first=0, last=PAIRS):
     lane = lax.broadcasted_iota(jnp.int32, (ROWS, 128), 1)
     table = out_pieces()
 
-    @pl.loop(0, PAIRS)
+    @pl.loop(first, last)
     def _(pair):
-        places = [place_of(owner, tab, pair, mat) for mat in range(10)]
         for chunk in range(27):
             out = None
             for (mat, j, turn), _lo, hi in reversed(table[chunk]):
-                val = back[pl.ds(places[mat] + j, ROWS, stride=CAP), :]
+                val = back[pl.ds(place[10 * pair + mat] + j, ROWS, stride=CAP), :]
                 if turn:
                     val = pltpu.roll(val, turn, 1)
                 out = val if out is None else jnp.where(lane < hi, val, out)
@@ -177,7 +191,7 @@
     first_out,
     basis_out,
     gram_out,
-    tab_out,
+    places_out,
     g2,
     m2,
     v2,
@@ -212,6 +226,7 @@
     second2,
     tab_vec,
     tab,
+    places,
     in_sem,
     send_sem,
     recv_sem,
@@ -221,36 +236,34 @@
     rank = lax.axis_index("tensor")
     my_y, my_z, my_c = me // 8, (me // 2) % 4, me % 2
 
-    def peer(t):
-        o = (11 * t) % 32
-        return (
-            ((my_y + o // 8) % 4) * 8 + ((my_z + (o // 2) % 4) % 4) * 2 + (my_c + o % 2) % 2
+    def peer(offset):
+        dy, dz, dc = offset
+        return ((my_y + dy) % 4) * 8 + ((my_z + dz) % 4) * 2 + (my_c + dc) % 2
+
+    def local(src, dst, n):
+        made = pltpu.make_async_copy(src, dst, in_sem.at[n])
+        made.start()
+        return made
+
+    load_q = local(q_hbm.at[:, 0, :], q2, 0)
+    barrier = pltpu.get_barrier_semaphore()
+
+    for offset in ORDER:
+        pl.semaphore_signal(
+            barrier, inc=1, device_id=(peer(offset), rank), device_id_type=MESH
         )
-
-    barrier = pltpu.get_barrier_semaphore()
-
-    @pl.loop(1, N_SHARD)
-    def _(t):
-        pl.semaphore_signal(barrier, inc=1, device_id=(peer(t), rank), device_id_type=MESH)
 
     for dx in range(1, N_TENSOR):
         pl.semaphore_signal(
             barrier, inc=1, device_id=(me, (rank + dx) % N_TENSOR), device_id_type=MESH
         )
 
-    def local(src, dst, n):
-        made = pltpu.make_async_copy(src, dst, in_sem.at[n])
-        made.start()
-        return made
-
-    load_q = local(q_hbm.at[:, 0, :], q2, 0)
     load_g = local(g_hbm, g2, 1)
     load_s = local(s_hbm.at[:, 0, :], s2, 2)
     load_m = local(m_hbm, m2, 3)
     load_v = local(v_hbm, v2, 4)
     tab_vec[...] = table_of(owners[...])
     load_tab = local(tab_vec, tab, 5)
-    save_tab = local(tab_vec, tab_out, 6)
 
     lined[ZERO_CHUNK] = jnp.zeros((ROWS, 128), F32)
     lined_q[ZERO_MAT] = jnp.zeros((ROWS, 128), F32)
@@ -262,9 +275,8 @@
     def exchange(send, recv, unit, n, off=0, rows=None):
         rows = unit if rows is None else rows
 
-        @pl.loop(1, N_SHARD)
-        def _(t):
-            dst = peer(t)
+        for offset in ORDER:
+            dst = peer(offset)
             pltpu.make_async_remote_copy(
                 src_ref=send.at[pl.ds(pl.multiple_of(dst * unit + off, 8), rows)],
                 dst_ref=recv.at[pl.ds(pl.multiple_of(me * unit + off, 8), rows)],
@@ -305,17 +317,19 @@
 
     load_q.wait()
     align_mats(q2, lined_q)
+    load_tab.wait()
+    pack_mats(lined_q, send_q)
+    pl.semaphore_wait(barrier, N_SHARD - 1 + N_TENSOR - 1)
+    exchange(send_q, qx.at[rank], QMSG, 0)
+
     load_g.wait()
     align_rows(g2, lined)
-    load_tab.wait()
-    pack_mats(lined_q, send_q)
     pack(lined, send_g)
+    exchange(send_g, recv_g, MSG, 1)
+
     load_s.wait()
     align_mats(s2, lined_q)
     pack_mats(lined_q, send_s)
-    pl.semaphore_wait(barrier, N_SHARD - 1 + N_TENSOR - 1)
-    exchange(send_q, qx.at[rank], QMSG, 0)
-    exchange(send_g, recv_g, MSG, 1)
     exchange(send_s, recv_s, QMSG, 2)
 
     load_m.wait()
@@ -330,6 +344,13 @@
     pack(lined, send_v)
     exchange(send_v, recv_v, MSG, 4, 0, HEAD)
     exchange(send_v, recv_v, MSG, 10, HEAD, TAIL)
+
+    @pl.loop(0, PAIRS)
+    def _(pair):
+        for mat in range(10):
+            places[10 * pair + mat] = place_of(owner, tab, pair, mat)
+
+    save_places = local(places, places_out, 6)
 
     def spread(src_of, dst_of, n):
         for dx in range(1, N_TENSOR):
@@ -476,16 +497,15 @@
     def write_second(here, val):
         second2[here, :] = val
 
-    unpack(back_n, owner, tab, write_second)
+    unpack(back_n, places, write_second)
     save_second = local(second2, second_out, 10)
-    for save in (save_tab, save_first, save_basis, save_gram, save_second):
+    for save in (save_places, save_first, save_basis, save_gram, save_second):
         save.wait()
     exchange_done(ret_d, back_d, MSG, 9)
 
 
 def unpack_kernel(
-    owner,
-    tab,
+    places,
     back_d,
     w_hbm,
     second,
@@ -504,12 +524,14 @@
     bias_w_out,
     bias_m_out,
     bias_v_out,
+    place,
     dv,
     w2,
     n2,
     f2,
     b2,
     s2,
+    bias,
     sem,
     sem_out,
 ):
@@ -518,8 +540,12 @@
         made.start()
         return made
 
-    load_d = copy(back_d, dv, 0)
-    load_w = copy(w_hbm, w2, 1)
+    load_p = copy(places, place, 0)
+    load_d = copy(back_d, dv, 1)
+    load_w = copy(w_hbm, w2, 2)
+    loads = [
+        copy(src, bias.at[n, 0], 3 + n) for n, src in enumerate((bias_g, bias_w, bias_m, bias_v))
+    ]
     passed = []
     for n, (src, held, dst) in enumerate(
         (
@@ -529,28 +555,33 @@
             (gram, s2, gram_out),
         )
     ):
-        passed.append((copy(src, held, 2 + n), held, dst))
-
-    moment = 0.9 * bias_m[...] + 0.1 * bias_g[...]
-    moment_two = 0.95 * bias_v[...] + 0.05 * bias_g[...] * bias_g[...]
-    bias_m_out[...] = moment
-    bias_v_out[...] = moment_two
-    bias_w_out[...] = bias_w[...] - 0.01 * (
-        moment / CORR_ONE / (jnp.sqrt(moment_two / CORR_TWO) + 1e-08)
-    )
+        passed.append((copy(src, held, 7 + n), held, dst))
+
+    for load in loads:
+        load.wait()
+    moment = 0.9 * bias[2] + 0.1 * bias[0]
+    moment_two = 0.95 * bias[3] + 0.05 * bias[0] * bias[0]
+    bias[5] = moment
+    bias[6] = moment_two
+    bias[4] = bias[1] - 0.01 * (moment / CORR_ONE / (jnp.sqrt(moment_two / CORR_TWO) + 1e-08))
+    saves = [
+        copy(bias.at[4 + n, 0], dst, n, sem_out)
+        for n, dst in enumerate((bias_w_out, bias_m_out, bias_v_out))
+    ]
 
     def write_weight(here, val):
         w = w2[here, :]
         w2[here, :] = w - 0.01 * (val + 0.1 * w)
 
+    load_p.wait()
     load_d.wait()
     load_w.wait()
-    saves = []
+    unpack(dv, place, write_weight, 0, PAIRS // 2)
     for n, (load, held, dst) in enumerate(passed):
         load.wait()
-        saves.append(copy(held, dst, n, sem_out))
-    unpack(dv, owner, tab, write_weight)
-    saves.append(copy(w2, weight_out, 4, sem_out))
+        saves.append(copy(held, dst, 3 + n, sem_out))
+    unpack(dv, place, write_weight, PAIRS // 2, PAIRS)
+    saves.append(copy(w2, weight_out, 7, sem_out))
     for save in saves:
         save.wait()
 
@@ -586,7 +617,7 @@
     tab_shape = (N_SHARD, 128)
     flat_q = (ROWS * QLINE, 1, 128)
     owner = owner_table.T
-    back_d, second, first, basis, gram, tab = pl.pallas_call(
+    back_d, second, first, basis, gram, places = pl.pallas_call(
         main_kernel,
         out_shape=(
             wide_out,
@@ -594,7 +625,7 @@
             flat_out,
             strip_out,
             strip_out,
-            jax.ShapeDtypeStruct(tab_shape, jnp.int32),
+            jax.ShapeDtypeStruct((128,), jnp.int32),
         ),
         in_specs=[smem, vmem] + [hbm] * 5,
         out_specs=(hbm,) * 6,
@@ -613,6 +644,7 @@
         + [strips] * 2
         + [wide, rows]
         + [pltpu.VMEM(tab_shape, jnp.int32), pltpu.SMEM(tab_shape, jnp.int32)]
+        + [pltpu.SMEM((128,), jnp.int32)]
         + [pltpu.SemaphoreType.DMA((n,)) for n in (11, 12, 12, 12)],
         compiler_params=pltpu.CompilerParams(
             collective_id=0, has_side_effects=True, vmem_limit_bytes=VMEM_ALL
@@ -623,17 +655,17 @@
     outs = pl.pallas_call(
         unpack_kernel,
         out_shape=(flat_out,) * 3 + (strip_out,) * 2 + (bias_out,) * 3,
-        in_specs=[smem] * 2 + [hbm] * 6 + [vmem] * 4,
-        out_specs=(hbm,) * 5 + (vmem,) * 3,
-        scratch_shapes=[wide]
+        in_specs=[hbm] * 11,
+        out_specs=(hbm,) * 8,
+        scratch_shapes=[pltpu.SMEM((128,), jnp.int32), wide]
         + [rows] * 3
         + [strips] * 2
-        + [pltpu.SemaphoreType.DMA((6,)), pltpu.SemaphoreType.DMA((5,))],
+        + [pltpu.VMEM((7, 1) + bias_gradient.shape, F32)]
+        + [pltpu.SemaphoreType.DMA((11,)), pltpu.SemaphoreType.DMA((8,))],
         compiler_params=pltpu.CompilerParams(vmem_limit_bytes=VMEM_ALL),
         name="unpack",
     )(
-        owner,
-        tab,
+        places,
         back_d,
         w,
         second,

time: 94.4 us -> 88.1 us (0.933)
  Pallas kernels: 93.6 us -> 87.3 us
    pallas_call x1, Pallas kernels: 87.6 us -> 83.3 us  [body(): pl.pallas_call(main_kernel, out_shape=(wide_out, flat_out, flat_out, stri...]
    pallas_call x1, Pallas kernels: 5.98 us -> 3.99 us  [body(): pl.pallas_call(unpack_kernel, out_shape=(flat_out,) * 3 + (strip_out,) *...]
where the time goes in v3:
time: 88.1 us; the launch traced here: 87.9 us
  Pallas kernels  87.3 us (99%)
    pallas_call x1, Pallas kernels, body(): pl.pallas_call(main_kernel, out_shape=(wide_out, flat_out, flat_out, stri...  83.3 us
    pallas_call x1, Pallas kernels, body(): pl.pallas_call(unpack_kernel, out_shape=(flat_out,) * 3 + (strip_out,) *...  3.99 us

profile of v3, /device:TPU:1, one launch (start us, length us, event | category | flops | bytes accessed | tf_op | source)
XLA Modules:
  0.0 87.9 jit_solution(18329705897994833828)
XLA Ops:
  0.6 83.3 %exchange_and_rotate.1 = (f32[2304,128]{1,0:T(8,128)}, f32[1944,128]{1,0:T(8,128)}, f32[1944,128]{1,0:T(8,128)}, f32[2,96,384]{2,1,0:T(8,128)}, f32[2,96,384]{2,1,0:T(8,128)}, /*index=5*/s32[128]{0:T(128)}) custom-call(s32[5,12]{1,0:T(8,128)} %bitcast.22, s32[5,12]{1,0:T(8,128)} %bitcast.23, f32[1944,128]{1,0:T(8,128)} %bitcast.16, f32[1944,128]{1,0:T(8,128)} %bitcast.17, ...), custom_call_target="tpu_custom_call" | custom-call | tf_op jit(solution)/shard_map/exchange_and_rotate/pallas_call | solution.py:620
  83.9 4.0 %unpack.1 = (f32[1944,128]{1,0:T(8,128)}, f32[1944,128]{1,0:T(8,128)}, f32[1944,128]{1,0:T(8,128)}, f32[2,96,384]{2,1,0:T(8,128)}, f32[2,96,384]{2,1,0:T(8,128)}...) custom-call(s32[128]{0:T(128)} %get-tuple-element.22.places, f32[2304,128]{1,0:T(8,128)} %get-tuple-element.23.back_d, ...), custom_call_target="tpu_custom_call" | custom-call | tf_op jit(solution)/shard_map/unpack/pallas_call | solution.py:655

commit v4 on v3

--- a/solution.py
+++ b/solution.py
@@ -21,7 +21,7 @@
 CHUNK_START = (0, 3, 4, 7, 10)
 CAP = 6
 MSG = ROWS * CAP
-QMSG = ROWS * 2
+QMSG = ROWS * 3
 LINE = 162
 QLINE = 45
 ZERO_CHUNK = 180
@@ -179,8 +179,7 @@
 
 
 def main_kernel(
-    owner,
-    owners,
+    owner_hbm,
     g_hbm,
     m_hbm,
     v_hbm,
@@ -199,15 +198,16 @@
     s2,
     lined,
     lined_q,
+    lined_s,
     send_g,
     send_m,
     send_v,
-    send_q,
-    send_s,
+    send_qs,
     recv_g,
     recv_m,
     recv_v,
-    recv_s,
+    recv_qs,
+    nat,
     qx,
     ret_d,
     ret_n,
@@ -224,6 +224,8 @@
     basis_strip,
     back_n,
     second2,
+    owner,
+    owners,
     tab_vec,
     tab,
     places,
@@ -245,7 +247,10 @@
         made.start()
         return made
 
+    load_owner = local(owner_hbm, owner, 11)
+    load_owners = local(owner_hbm, owners, 12)
     load_q = local(q_hbm.at[:, 0, :], q2, 0)
+    load_s = local(s_hbm.at[:, 0, :], s2, 2)
     barrier = pltpu.get_barrier_semaphore()
 
     for offset in ORDER:
@@ -259,14 +264,16 @@
         )
 
     load_g = local(g_hbm, g2, 1)
-    load_s = local(s_hbm.at[:, 0, :], s2, 2)
     load_m = local(m_hbm, m2, 3)
     load_v = local(v_hbm, v2, 4)
+    load_owner.wait()
+    load_owners.wait()
     tab_vec[...] = table_of(owners[...])
     load_tab = local(tab_vec, tab, 5)
 
     lined[ZERO_CHUNK] = jnp.zeros((ROWS, 128), F32)
     lined_q[ZERO_MAT] = jnp.zeros((ROWS, 128), F32)
+    lined_s[ZERO_MAT] = jnp.zeros((ROWS, 128), F32)
 
     def own_copy(send, recv, unit, off, rows, n):
         own = pl.ds(pl.multiple_of(me * unit + off, 8), rows)
@@ -309,28 +316,45 @@
             for k in range(CAP):
                 send[pl.ds(MSG * d + k, ROWS, stride=CAP), :] = lines[tab[d, k]]
 
-    def pack_mats(lines, send):
+    def mats_copy():
+        return pltpu.make_async_copy(send_qs.at[me], recv_qs.at[me], own_sem.at[0])
+
+    def pack_mats():
+        lane = lax.broadcasted_iota(jnp.int32, (ROWS, 128), 1)
+
         @pl.loop(0, N_SHARD)
         def _(d):
-            for j in range(2):
-                send[pl.ds(QMSG * d + j, ROWS, stride=2), :] = lines[tab[d, 8 + j]]
+            one, two = tab[d, 8], tab[d, 9]
+            q_two = pltpu.roll(lined_q[two], 96, 1)
+            s_one = pltpu.roll(lined_s[one], 64, 1)
+            s_two = pltpu.roll(lined_s[two], 32, 1)
+            send_qs[d, pl.ds(0, ROWS, stride=3), :] = jnp.where(lane < 96, lined_q[one], q_two)
+            send_qs[d, pl.ds(1, ROWS, stride=3), :] = jnp.where(lane < 64, q_two, s_one)
+            send_qs[d, pl.ds(2, ROWS, stride=3), :] = jnp.where(lane < 32, s_one, s_two)
 
     load_q.wait()
     align_mats(q2, lined_q)
+    load_s.wait()
+    align_mats(s2, lined_s)
     load_tab.wait()
-    pack_mats(lined_q, send_q)
+    pack_mats()
     pl.semaphore_wait(barrier, N_SHARD - 1 + N_TENSOR - 1)
-    exchange(send_q, qx.at[rank], QMSG, 0)
+    for offset in ORDER:
+        dst = peer(offset)
+        pltpu.make_async_remote_copy(
+            src_ref=send_qs.at[dst],
+            dst_ref=recv_qs.at[me],
+            send_sem=send_sem.at[0],
+            recv_sem=recv_sem.at[0],
+            device_id=(dst, rank),
+            device_id_type=MESH,
+        ).start()
+    mats_copy().start()
 
     load_g.wait()
     align_rows(g2, lined)
     pack(lined, send_g)
     exchange(send_g, recv_g, MSG, 1)
-
-    load_s.wait()
-    align_mats(s2, lined_q)
-    pack_mats(lined_q, send_s)
-    exchange(send_s, recv_s, QMSG, 2)
 
     load_m.wait()
     m2[...] = 0.9 * m2[...] + 0.1 * g2[...]
@@ -376,7 +400,23 @@
         every.wait_send()
         every.wait_recv()
 
-    exchange_done(send_q, qx.at[rank], QMSG, 0)
+    most = pl.ds(0, N_SHARD - 1)
+    every_mat = pltpu.make_async_remote_copy(
+        src_ref=send_qs.at[most],
+        dst_ref=recv_qs.at[most],
+        send_sem=send_sem.at[0],
+        recv_sem=recv_sem.at[0],
+        device_id=((me + 1) % N_SHARD, rank),
+        device_id_type=MESH,
+    )
+    mats_copy().wait()
+    every_mat.wait_send()
+    every_mat.wait_recv()
+    for k in range(3):
+        into = nat if k == 2 else qx.at[rank, k]
+        for s in range(0, N_SHARD, 2):
+            pair = [recv_qs[s + n, pl.ds(k, ROWS, stride=3), :] for n in range(2)]
+            into[pl.ds(ROWS * s, 2 * ROWS), :] = jnp.concatenate(pair, axis=0)
     q_part = (lambda other: qx.at[rank]), (lambda other: qx.at[other])
     spread(*q_part, 5)
 
@@ -405,7 +445,12 @@
     spread_done(qx.at[pl.ds(0, 3)], 5)
     lane = lax.broadcasted_iota(jnp.int32, (D, 128), 1)
     for j in range(2):
-        parts = [qx[x, pl.ds(j, D, stride=2), :] for x in range(4)]
+        parts = [qx[x, 0] for x in range(4)]
+        if j == 1:
+            parts = [
+                pltpu.roll(jnp.where(lane >= 96, part, qx[x, 1]), 32, 1)
+                for x, part in enumerate(parts)
+            ]
         full = jnp.concatenate(
             [
                 jnp.where(lane < 96, parts[0], pltpu.roll(parts[1], 96, 1)),
@@ -417,7 +462,6 @@
         q_hi[j], q_lo[j] = split(full)
         qt_hi[j], qt_lo[j] = split(full.T)
 
-    exchange_done(send_s, recv_s, QMSG, 2)
     exchange_done(send_m, recv_m, MSG, 3)
 
     @pl.loop(0, CAP)
@@ -431,11 +475,15 @@
         m_hat[pl.ds(k, D, stride=CAP), :] = hat[:, 128:]
 
     spread_done(xg.at[pl.ds(0, 3)], 6)
+    gram_parts = (
+        pltpu.roll(jnp.where(lane >= 64, qx[rank, 1], nat[...]), 64, 1),
+        pltpu.roll(nat[...], 96, 1),
+    )
     for j in range(2):
         total = gram[j, strip(rank), :]
         for dx in range(1, N_TENSOR):
             total = total + xg[(rank + dx) % N_TENSOR, j]
-        held = recv_s[pl.ds(j, D, stride=2), :].T[:96]
+        held = gram_parts[j].T[:96]
         fresh = 0.95 * held + 0.05 * total
         gram_strip[j] = fresh
         power[j, strip(rank), :] = dot3(split(fresh), (q_hi[j], q_lo[j]), NN)
@@ -557,6 +605,14 @@
     ):
         passed.append((copy(src, held, 7 + n), held, dst))
 
+    def write_weight(here, val):
+        w = w2[here, :]
+        w2[here, :] = w - 0.01 * (val + 0.1 * w)
+
+    load_p.wait()
+    load_d.wait()
+    load_w.wait()
+    unpack(dv, place, write_weight, 0, PAIRS // 2)
     for load in loads:
         load.wait()
     moment = 0.9 * bias[2] + 0.1 * bias[0]
@@ -568,15 +624,6 @@
         copy(bias.at[4 + n, 0], dst, n, sem_out)
         for n, dst in enumerate((bias_w_out, bias_m_out, bias_v_out))
     ]
-
-    def write_weight(here, val):
-        w = w2[here, :]
-        w2[here, :] = w - 0.01 * (val + 0.1 * w)
-
-    load_p.wait()
-    load_d.wait()
-    load_w.wait()
-    unpack(dv, place, write_weight, 0, PAIRS // 2)
     for n, (load, held, dst) in enumerate(passed):
         load.wait()
         saves.append(copy(held, dst, 3 + n, sem_out))
@@ -599,13 +646,12 @@
     bias_first,
     bias_second,
 ):
-    smem = pl.BlockSpec(memory_space=pltpu.SMEM)
-    vmem = pl.BlockSpec(memory_space=pltpu.VMEM)
     hbm = pl.BlockSpec(memory_space=pltpu.HBM)
     flat = (ROWS * LINE, 128)
     g, w, m, v = (a.reshape(flat) for a in (gradient, weight, first_moment, second_moment))
     wide = pltpu.VMEM((N_SHARD * MSG, 128), F32)
-    mats = pltpu.VMEM((N_SHARD * QMSG, 128), F32)
+    mats = pltpu.VMEM((N_SHARD, QMSG, 128), F32)
+    lines_q = pltpu.VMEM((ZERO_MAT + 1, ROWS, 128), F32)
     full = pltpu.VMEM((2, D, D), F32)
     half = pltpu.VMEM((2, D, D), BF16)
     strips = pltpu.VMEM((2, 96, D), F32)
@@ -627,30 +673,31 @@
             strip_out,
             jax.ShapeDtypeStruct((128,), jnp.int32),
         ),
-        in_specs=[smem, vmem] + [hbm] * 5,
+        in_specs=[hbm] * 6,
         out_specs=(hbm,) * 6,
         scratch_shapes=[rows] * 3
         + [rows_q] * 2
-        + [pltpu.VMEM((ZERO_CHUNK + 1, ROWS, 128), F32), pltpu.VMEM((ZERO_MAT + 1, ROWS, 128), F32)]
-        + [wide] * 3
-        + [mats] * 2
+        + [pltpu.VMEM((ZERO_CHUNK + 1, ROWS, 128), F32), lines_q, lines_q]
         + [wide] * 3
         + [mats]
-        + [pltpu.VMEM((N_TENSOR, N_SHARD * QMSG, 128), F32)]
+        + [wide] * 3
+        + [mats, pltpu.VMEM((D, 128), F32)]
+        + [pltpu.VMEM((N_TENSOR, 2, D, 128), F32)]
         + [wide] * 2
         + [full, pltpu.VMEM((N_TENSOR, 2, 96, D), F32), full]
         + [half] * 4
         + [wide] * 2
         + [strips] * 2
         + [wide, rows]
+        + [pltpu.SMEM(owner.shape, jnp.int32), pltpu.VMEM(owner.shape, jnp.int32)]
         + [pltpu.VMEM(tab_shape, jnp.int32), pltpu.SMEM(tab_shape, jnp.int32)]
         + [pltpu.SMEM((128,), jnp.int32)]
-        + [pltpu.SemaphoreType.DMA((n,)) for n in (11, 12, 12, 12)],
+        + [pltpu.SemaphoreType.DMA((n,)) for n in (13, 12, 12, 12)],
         compiler_params=pltpu.CompilerParams(
             collective_id=0, has_side_effects=True, vmem_limit_bytes=VMEM_ALL
         ),
         name="exchange_and_rotate",
-    )(owner, owner, g, m, v, left_basis.reshape(flat_q), left_gram.reshape(flat_q))
+    )(owner, g, m, v, left_basis.reshape(flat_q), left_gram.reshape(flat_q))
     bias_out = jax.ShapeDtypeStruct(bias_gradient.shape, F32)
     outs = pl.pallas_call(
         unpack_kernel,

time: 88.1 us -> 92.2 us (1.047)
  the two profiles are of different devices: /device:TPU:1 before, /device:TPU:25 now
where the time goes in v4:
time: 92.2 us; the launch traced here: 92.1 us
  Pallas kernels  91.5 us (99%)
    pallas_call x1, Pallas kernels, body(): pl.pallas_call(main_kernel, out_shape=(wide_out, flat_out, flat_out, stri...  87.4 us
    pallas_call x1, Pallas kernels, body(): pl.pallas_call(unpack_kernel, out_shape=(flat_out,) * 3 + (strip_out,) *...  4.03 us

profile of v4, /device:TPU:25, one launch (start us, length us, event | category | flops | bytes accessed | tf_op | source)
XLA Modules:
  0.0 92.1 jit_solution(2288523679417681106)
XLA Ops:
  0.6 87.4 %exchange_and_rotate.1 = (f32[2304,128]{1,0:T(8,128)}, f32[1944,128]{1,0:T(8,128)}, f32[1944,128]{1,0:T(8,128)}, f32[2,96,384]{2,1,0:T(8,128)}, f32[2,96,384]{2,1,0:T(8,128)}, /*index=5*/s32[128]{0:T(128)}) custom-call(s32[5,12]{1,0:T(8,128)} %bitcast.22, f32[1944,128]{1,0:T(8,128)} %bitcast.17, f32[1944,128]{1,0:T(8,128)} %bitcast.18, ...), custom_call_target="tpu_custom_call" | custom-call | tf_op jit(solution)/shard_map/exchange_and_rotate/pallas_call | solution.py:666
  88.1 4.0 %unpack.1 = (f32[1944,128]{1,0:T(8,128)}, f32[1944,128]{1,0:T(8,128)}, f32[1944,128]{1,0:T(8,128)}, f32[2,96,384]{2,1,0:T(8,128)}, f32[2,96,384]{2,1,0:T(8,128)}...) custom-call(s32[128]{0:T(128)} %get-tuple-element.22.places, f32[2304,128]{1,0:T(8,128)} %get-tuple-element.23.back_d, ...), custom_call_target="tpu_custom_call" | custom-call | tf_op jit(solution)/shard_map/unpack/pallas_call | solution.py:702

commit v5 on v4

--- a/solution.py
+++ b/solution.py
@@ -137,6 +137,15 @@
 
 NN = ((1,), (0,))
 NT = ((1,), (1,))
+
+
+def outer3(pieces):
+    high, low = pieces
+    dot = functools.partial(
+        lax.dot_general, dimension_numbers=(NT, ((), ())), preferred_element_type=F32
+    )
+    mixed = dot(high, low)
+    return dot(high, high) + (mixed + mixed.T)
 
 
 def out_pieces():
@@ -281,7 +290,6 @@
 
     def exchange(send, recv, unit, n, off=0, rows=None):
         rows = unit if rows is None else rows
-
         for offset in ORDER:
             dst = peer(offset)
             pltpu.make_async_remote_copy(
@@ -292,13 +300,11 @@
                 device_id=(dst, rank),
                 device_id_type=MESH,
             ).start()
-
         own_copy(send, recv, unit, off, rows, n).start()
 
-    def exchange_done(send, recv, unit, n, off=0, rows=None):
-        rows = unit if rows is None else rows
-        whole = pl.ds(0, (N_SHARD - 1) * rows)
-        every = pltpu.make_async_remote_copy(
+    def share(send, recv, rows, count, n):
+        whole = pl.ds(0, count * rows)
+        return pltpu.make_async_remote_copy(
             src_ref=send.at[whole],
             dst_ref=recv.at[whole],
             send_sem=send_sem.at[n],
@@ -306,7 +312,11 @@
             device_id=((me + 1) % N_SHARD, rank),
             device_id_type=MESH,
         )
+
+    def exchange_done(send, recv, unit, n, off=0, rows=None):
+        rows = unit if rows is None else rows
         own_copy(send, recv, unit, off, rows, n).wait()
+        every = share(send, recv, rows, N_SHARD - 1, n)
         every.wait_send()
         every.wait_recv()
 
@@ -322,15 +332,20 @@
     def pack_mats():
         lane = lax.broadcasted_iota(jnp.int32, (ROWS, 128), 1)
 
-        @pl.loop(0, N_SHARD)
-        def _(d):
-            one, two = tab[d, 8], tab[d, 9]
-            q_two = pltpu.roll(lined_q[two], 96, 1)
-            s_one = pltpu.roll(lined_s[one], 64, 1)
-            s_two = pltpu.roll(lined_s[two], 32, 1)
-            send_qs[d, pl.ds(0, ROWS, stride=3), :] = jnp.where(lane < 96, lined_q[one], q_two)
-            send_qs[d, pl.ds(1, ROWS, stride=3), :] = jnp.where(lane < 64, q_two, s_one)
-            send_qs[d, pl.ds(2, ROWS, stride=3), :] = jnp.where(lane < 32, s_one, s_two)
+        @pl.loop(0, N_SHARD // 8)
+        def _(step):
+            held = []
+            for n in range(8):
+                one, two = tab[8 * step + n, 8], tab[8 * step + n, 9]
+                held.append((lined_q[one], lined_q[two], lined_s[one], lined_s[two]))
+            for n, (q_one, q_two, s_one, s_two) in enumerate(held):
+                d = 8 * step + n
+                q_two = pltpu.roll(q_two, 96, 1)
+                s_one = pltpu.roll(s_one, 64, 1)
+                s_two = pltpu.roll(s_two, 32, 1)
+                send_qs[d, pl.ds(0, ROWS, stride=3), :] = jnp.where(lane < 96, q_one, q_two)
+                send_qs[d, pl.ds(1, ROWS, stride=3), :] = jnp.where(lane < 64, q_two, s_one)
+                send_qs[d, pl.ds(2, ROWS, stride=3), :] = jnp.where(lane < 32, s_one, s_two)
 
     load_q.wait()
     align_mats(q2, lined_q)
@@ -412,29 +427,30 @@
     mats_copy().wait()
     every_mat.wait_send()
     every_mat.wait_recv()
+    lane = lax.broadcasted_iota(jnp.int32, (D, 128), 1)
+    lane_half = lax.broadcasted_iota(jnp.int32, (D // 2, 128), 1)
     for k in range(3):
-        into = nat if k == 2 else qx.at[rank, k]
         for s in range(0, N_SHARD, 2):
             pair = [recv_qs[s + n, pl.ds(k, ROWS, stride=3), :] for n in range(2)]
-            into[pl.ds(ROWS * s, 2 * ROWS), :] = jnp.concatenate(pair, axis=0)
+            into = jnp.concatenate(pair, axis=0)
+            if k == 0:
+                qx[rank, pl.ds(ROWS * s, 2 * ROWS), :] = into
+            else:
+                nat[k - 1, pl.ds(ROWS * s, 2 * ROWS), :] = into
+    qx[rank, pl.ds(D, D // 2), :] = jnp.where(
+        lane_half < 64, nat[0, : D // 2], pltpu.roll(nat[0, D // 2 :], 64, 1)
+    )
     q_part = (lambda other: qx.at[rank]), (lambda other: qx.at[other])
     spread(*q_part, 5)
 
     exchange_done(send_g, recv_g, MSG, 1)
     c0 = tab[me, 10]
     for j in range(2):
-        left_h, left_l, right_h, right_l = [], [], [], []
+        chunks = []
         for k in range(CAP):
-            chunk = recv_g[pl.ds(k, D, stride=CAP), :]
             mine = (k < c0) if j == 0 else (k >= c0)
-            high, low = split(chunk)
-            right_h.append(high)
-            right_l.append(low)
-            high, low = split(jnp.where(mine, chunk, 0.0))
-            left_h.append(high)
-            left_l.append(low)
-        cat = functools.partial(jnp.concatenate, axis=1)
-        gram[j] = dot3((cat(left_h), cat(left_l)), (cat(right_h), cat(right_l)), NT)
+            chunks.append(split(jnp.where(mine, recv_g[pl.ds(k, D, stride=CAP), :], 0.0)))
+        gram[j] = outer3(tuple(jnp.concatenate(half, axis=1) for half in zip(*chunks)))
 
     def strip(x):
         return pl.ds(pl.multiple_of(96 * x, 8), 96)
@@ -443,13 +459,14 @@
     spread(*g_part, 6)
 
     spread_done(qx.at[pl.ds(0, 3)], 5)
-    lane = lax.broadcasted_iota(jnp.int32, (D, 128), 1)
     for j in range(2):
-        parts = [qx[x, 0] for x in range(4)]
+        parts = [qx[x, :D] for x in range(4)]
         if j == 1:
+            rests = [qx[x, D:] for x in range(4)]
+            rests = [jnp.concatenate([r, pltpu.roll(r, 64, 1)], axis=0) for r in rests]
             parts = [
-                pltpu.roll(jnp.where(lane >= 96, part, qx[x, 1]), 32, 1)
-                for x, part in enumerate(parts)
+                pltpu.roll(jnp.where(lane >= 96, part, rest), 32, 1)
+                for part, rest in zip(parts, rests)
             ]
         full = jnp.concatenate(
             [
@@ -476,8 +493,8 @@
 
     spread_done(xg.at[pl.ds(0, 3)], 6)
     gram_parts = (
-        pltpu.roll(jnp.where(lane >= 64, qx[rank, 1], nat[...]), 64, 1),
-        pltpu.roll(nat[...], 96, 1),
+        pltpu.roll(jnp.where(lane >= 64, nat[0], nat[1]), 64, 1),
+        pltpu.roll(nat[1], 96, 1),
     )
     for j in range(2):
         total = gram[j, strip(rank), :]
@@ -522,20 +539,18 @@
         norm = jnp.sqrt(jnp.sum(full * full, keepdims=True) + 1e-06)
         power[j] = full / norm
 
-    @pl.loop(0, NS_STEPS)
+    @pl.loop(0, NS_STEPS - 1)
     def _(sweep):
         for j in range(2):
             frame = power[j]
             pieces = split(frame)
-            square = dot3(pieces, pieces, NT)
-            power[j] = 1.5 * frame - 0.5 * dot3(split(square), pieces, NN)
-
-    for x in range(N_TENSOR):
-
-        @pl.when(rank == x)
-        def _():
-            for j in range(2):
-                basis_strip[j] = power[j, :, 96 * x : 96 * x + 96].T
+            power[j] = 1.5 * frame - 0.5 * dot3(split(outer3(pieces)), pieces, NN)
+
+    for j in range(2):
+        gram[j] = power[j].T
+        square = split(outer3(split(power[j])))
+        mine = gram[j, strip(rank), :]
+        basis_strip[j] = 1.5 * mine - 0.5 * dot3(split(mine), square, NN)
 
     save_basis = local(basis_strip, basis_out, 8)
     save_gram = local(gram_strip, gram_out, 9)
@@ -681,8 +696,8 @@
         + [wide] * 3
         + [mats]
         + [wide] * 3
-        + [mats, pltpu.VMEM((D, 128), F32)]
-        + [pltpu.VMEM((N_TENSOR, 2, D, 128), F32)]
+        + [mats, pltpu.VMEM((2, D, 128), F32)]
+        + [pltpu.VMEM((N_TENSOR, D + D // 2, 128), F32)]
         + [wide] * 2
         + [full, pltpu.VMEM((N_TENSOR, 2, 96, D), F32), full]
         + [half] * 4

time: 92.2 us -> 86.9 us (0.943)
  Pallas kernels: 91.5 us -> 86.1 us
    pallas_call x1, Pallas kernels: 87.4 us -> 82.1 us  [body(): pl.pallas_call(main_kernel, out_shape=(wide_out, flat_out, flat_out, stri...]
where the time goes in v5:
time: 86.9 us; the launch traced here: 86.8 us
  Pallas kernels  86.1 us (99%)
    pallas_call x1, Pallas kernels, body(): pl.pallas_call(main_kernel, out_shape=(wide_out, flat_out, flat_out, stri...  82.1 us
    pallas_call x1, Pallas kernels, body(): pl.pallas_call(unpack_kernel, out_shape=(flat_out,) * 3 + (strip_out,) *...  4.03 us

profile of v5, /device:TPU:25, one launch (start us, length us, event | category | flops | bytes accessed | tf_op | source)
XLA Modules:
  0.0 86.8 jit_solution(13299362887430555668)
XLA Ops:
  0.6 82.1 %exchange_and_rotate.1 = (f32[2304,128]{1,0:T(8,128)}, f32[1944,128]{1,0:T(8,128)}, f32[1944,128]{1,0:T(8,128)}, f32[2,96,384]{2,1,0:T(8,128)}, f32[2,96,384]{2,1,0:T(8,128)}, /*index=5*/s32[128]{0:T(128)}) custom-call(s32[5,12]{1,0:T(8,128)} %bitcast.22, f32[1944,128]{1,0:T(8,128)} %bitcast.17, f32[1944,128]{1,0:T(8,128)} %bitcast.18, ...), custom_call_target="tpu_custom_call" | custom-call | tf_op jit(solution)/shard_map/exchange_and_rotate/pallas_call | solution.py:681
  82.7 4.0 %unpack.1 = (f32[1944,128]{1,0:T(8,128)}, f32[1944,128]{1,0:T(8,128)}, f32[1944,128]{1,0:T(8,128)}, f32[2,96,384]{2,1,0:T(8,128)}, f32[2,96,384]{2,1,0:T(8,128)}...) custom-call(s32[128]{0:T(128)} %get-tuple-element.22.places, f32[2304,128]{1,0:T(8,128)} %get-tuple-element.23.back_d, ...), custom_call_target="tpu_custom_call" | custom-call | tf_op jit(solution)/shard_map/unpack/pallas_call | solution.py:717

commit v6 on v5

--- a/solution.py
+++ b/solution.py
@@ -126,26 +126,28 @@
     return high, (x - high.astype(F32)).astype(BF16)
 
 
-def dot3(a, b, dims):
+NN = ((1,), (0,))
+NT = ((1,), (1,))
+
+
+def dot(a, b, dims):
+    return lax.dot_general(a, b, (dims, ((), ())), preferred_element_type=F32)
+
+
+def dot3(a, b):
     ah, al = a
     bh, bl = b
-    dot = functools.partial(
-        lax.dot_general, dimension_numbers=(dims, ((), ())), preferred_element_type=F32
-    )
-    return dot(ah, bh) + (dot(ah, bl) + dot(al, bh))
-
-
-NN = ((1,), (0,))
-NT = ((1,), (1,))
+    wide = bh.shape[1]
+    both = dot(ah, jnp.concatenate([bh, bl], axis=1), NN)
+    return both[:, :wide] + (both[:, wide:] + dot(al, bh, NN))
 
 
 def outer3(pieces):
     high, low = pieces
-    dot = functools.partial(
-        lax.dot_general, dimension_numbers=(NT, ((), ())), preferred_element_type=F32
-    )
-    mixed = dot(high, low)
-    return dot(high, high) + (mixed + mixed.T)
+    wide = high.shape[0]
+    both = dot(high, jnp.concatenate([high, low], axis=0), NT)
+    mixed = both[:, wide:]
+    return both[:, :wide] + (mixed + mixed.T)
 
 
 def out_pieces():
@@ -275,14 +277,15 @@
     load_g = local(g_hbm, g2, 1)
     load_m = local(m_hbm, m2, 3)
     load_v = local(v_hbm, v2, 4)
+    lined[ZERO_CHUNK] = jnp.zeros((ROWS, 128), F32)
+    lined_q[ZERO_MAT] = jnp.zeros((ROWS, 128), F32)
+    lined_s[ZERO_MAT] = jnp.zeros((ROWS, 128), F32)
+    load_q.wait()
+    align_mats(q2, lined_q)
     load_owner.wait()
     load_owners.wait()
     tab_vec[...] = table_of(owners[...])
     load_tab = local(tab_vec, tab, 5)
-
-    lined[ZERO_CHUNK] = jnp.zeros((ROWS, 128), F32)
-    lined_q[ZERO_MAT] = jnp.zeros((ROWS, 128), F32)
-    lined_s[ZERO_MAT] = jnp.zeros((ROWS, 128), F32)
 
     def own_copy(send, recv, unit, off, rows, n):
         own = pl.ds(pl.multiple_of(me * unit + off, 8), rows)
@@ -347,8 +350,6 @@
                 send_qs[d, pl.ds(1, ROWS, stride=3), :] = jnp.where(lane < 64, q_two, s_one)
                 send_qs[d, pl.ds(2, ROWS, stride=3), :] = jnp.where(lane < 32, s_one, s_two)
 
-    load_q.wait()
-    align_mats(q2, lined_q)
     load_s.wait()
     align_mats(s2, lined_s)
     load_tab.wait()
@@ -487,7 +488,7 @@
         both = jnp.concatenate(
             [recv_g[pl.ds(k, D, stride=CAP), :], recv_m[pl.ds(k, D, stride=CAP), :]], axis=1
         )
-        hat = dot3((qt_hi[sel], qt_lo[sel]), split(both), NN)
+        hat = dot3((qt_hi[sel], qt_lo[sel]), split(both))
         g_hat[pl.ds(k, D, stride=CAP), :] = hat[:, :128]
         m_hat[pl.ds(k, D, stride=CAP), :] = hat[:, 128:]
 
@@ -503,7 +504,7 @@
         held = gram_parts[j].T[:96]
         fresh = 0.95 * held + 0.05 * total
         gram_strip[j] = fresh
-        power[j, strip(rank), :] = dot3(split(fresh), (q_hi[j], q_lo[j]), NN)
+        power[j, strip(rank), :] = dot3(split(fresh), (q_hi[j], q_lo[j]))
     p_part = (
         (lambda other: power.at[:, strip(rank), :]),
         (lambda other: power.at[:, strip(other), :]),
@@ -529,7 +530,7 @@
     @pl.loop(0, CAP)
     def _(k):
         sel = jnp.where(k >= c0, 1, 0)
-        ret_d[pl.ds(k, D, stride=CAP), :] = dot3((q_hi[sel], q_lo[sel]), split(m_hat[pl.ds(k, D, stride=CAP), :]), NN)
+        ret_d[pl.ds(k, D, stride=CAP), :] = dot3((q_hi[sel], q_lo[sel]), split(m_hat[pl.ds(k, D, stride=CAP), :]))
 
     exchange(ret_d, back_d, MSG, 9)
 
@@ -544,13 +545,13 @@
         for j in range(2):
             frame = power[j]
             pieces = split(frame)
-            power[j] = 1.5 * frame - 0.5 * dot3(split(outer3(pieces)), pieces, NN)
+            power[j] = 1.5 * frame - 0.5 * dot3(split(outer3(pieces)), pieces)
 
     for j in range(2):
         gram[j] = power[j].T
         square = split(outer3(split(power[j])))
         mine = gram[j, strip(rank), :]
-        basis_strip[j] = 1.5 * mine - 0.5 * dot3(split(mine), square, NN)
+        basis_strip[j] = 1.5 * mine - 0.5 * dot3(split(mine), square)
 
     save_basis = local(basis_strip, basis_out, 8)
     save_gram = local(gram_strip, gram_out, 9)
@@ -627,7 +628,13 @@
     load_p.wait()
     load_d.wait()
     load_w.wait()
-    unpack(dv, place, write_weight, 0, PAIRS // 2)
+    unpack(dv, place, write_weight, 0, 1)
+    saves = []
+    for n, (load, held, dst) in enumerate(passed):
+        load.wait()
+        saves.append(copy(held, dst, 3 + n, sem_out))
+    unpack(dv, place, write_weight, 1, PAIRS)
+    saves.append(copy(w2, weight_out, 7, sem_out))
     for load in loads:
         load.wait()
     moment = 0.9 * bias[2] + 0.1 * bias[0]
@@ -635,15 +642,10 @@
     bias[5] = moment
     bias[6] = moment_two
     bias[4] = bias[1] - 0.01 * (moment / CORR_ONE / (jnp.sqrt(moment_two / CORR_TWO) + 1e-08))
-    saves = [
+    saves += [
         copy(bias.at[4 + n, 0], dst, n, sem_out)
         for n, dst in enumerate((bias_w_out, bias_m_out, bias_v_out))
     ]
-    for n, (load, held, dst) in enumerate(passed):
-        load.wait()
-        saves.append(copy(held, dst, 3 + n, sem_out))
-    unpack(dv, place, write_weight, PAIRS // 2, PAIRS)
-    saves.append(copy(w2, weight_out, 7, sem_out))
     for save in saves:
         save.wait()
 

time: 86.9 us -> 87.9 us (1.012)
  Pallas kernels: 86.1 us -> 87.1 us
where the time goes in v6:
time: 87.9 us; the launch traced here: 87.8 us
  Pallas kernels  87.1 us (99%)
    pallas_call x1, Pallas kernels, body(): pl.pallas_call(main_kernel, out_shape=(wide_out, flat_out, flat_out, stri...  82.9 us
    pallas_call x1, Pallas kernels, body(): pl.pallas_call(unpack_kernel, out_shape=(flat_out,) * 3 + (strip_out,) *...  4.25 us

profile of v6, /device:TPU:25, one launch (start us, length us, event | category | flops | bytes accessed | tf_op | source)
XLA Modules:
  0.0 87.8 jit_solution(2797120369275887179)
XLA Ops:
  0.6 82.9 %exchange_and_rotate.1 = (f32[2304,128]{1,0:T(8,128)}, f32[1944,128]{1,0:T(8,128)}, f32[1944,128]{1,0:T(8,128)}, f32[2,96,384]{2,1,0:T(8,128)}, f32[2,96,384]{2,1,0:T(8,128)}, /*index=5*/s32[128]{0:T(128)}) custom-call(s32[5,12]{1,0:T(8,128)} %bitcast.22, f32[1944,128]{1,0:T(8,128)} %bitcast.17, f32[1944,128]{1,0:T(8,128)} %bitcast.18, ...), custom_call_target="tpu_custom_call" | custom-call | tf_op jit(solution)/shard_map/exchange_and_rotate/pallas_call | solution.py:683
  83.5 4.2 %unpack.1 = (f32[1944,128]{1,0:T(8,128)}, f32[1944,128]{1,0:T(8,128)}, f32[1944,128]{1,0:T(8,128)}, f32[2,96,384]{2,1,0:T(8,128)}, f32[2,96,384]{2,1,0:T(8,128)}...) custom-call(s32[128]{0:T(128)} %get-tuple-element.22.places, f32[2304,128]{1,0:T(8,128)} %get-tuple-element.23.back_d, ...), custom_call_target="tpu_custom_call" | custom-call | tf_op jit(solution)/shard_map/unpack/pallas_call | solution.py:719

commit v7 on v5

--- a/solution.py
+++ b/solution.py
@@ -546,6 +546,14 @@
             pieces = split(frame)
             power[j] = 1.5 * frame - 0.5 * dot3(split(outer3(pieces)), pieces, NN)
 
+    exchange_done(ret_n, back_n, MSG, 8, 0, HEAD)
+    exchange_done(ret_n, back_n, MSG, 11, HEAD, TAIL)
+
+    def write_second(here, val):
+        second2[here, :] = val
+
+    unpack(back_n, places, write_second)
+    save_second = local(second2, second_out, 10)
     for j in range(2):
         gram[j] = power[j].T
         square = split(outer3(split(power[j])))
@@ -554,17 +562,9 @@
 
     save_basis = local(basis_strip, basis_out, 8)
     save_gram = local(gram_strip, gram_out, 9)
-    exchange_done(ret_n, back_n, MSG, 8, 0, HEAD)
-    exchange_done(ret_n, back_n, MSG, 11, HEAD, TAIL)
-
-    def write_second(here, val):
-        second2[here, :] = val
-
-    unpack(back_n, places, write_second)
-    save_second = local(second2, second_out, 10)
+    exchange_done(ret_d, back_d, MSG, 9)
     for save in (save_places, save_first, save_basis, save_gram, save_second):
         save.wait()
-    exchange_done(ret_d, back_d, MSG, 9)
 
 
 def unpack_kernel(

time: 86.9 us -> 86.7 us (level)
  the two profiles are of different devices: /device:TPU:25 before, /device:TPU:1 now
where the time goes in v7:
time: 86.7 us; the launch traced here: 85 us
  Pallas kernels  84.4 us (97%)
    pallas_call x1, Pallas kernels, body(): pl.pallas_call(main_kernel, out_shape=(wide_out, flat_out, flat_out, stri...  80.4 us
    pallas_call x1, Pallas kernels, body(): pl.pallas_call(unpack_kernel, out_shape=(flat_out,) * 3 + (strip_out,) *...  4.03 us

profile of v7, /device:TPU:1, one launch (start us, length us, event | category | flops | bytes accessed | tf_op | source)
XLA Modules:
  0.0 85.0 jit_solution(11457605053324969873)
XLA Ops:
  0.6 80.4 %exchange_and_rotate.1 = (f32[2304,128]{1,0:T(8,128)}, f32[1944,128]{1,0:T(8,128)}, f32[1944,128]{1,0:T(8,128)}, f32[2,96,384]{2,1,0:T(8,128)}, f32[2,96,384]{2,1,0:T(8,128)}, /*index=5*/s32[128]{0:T(128)}) custom-call(s32[5,12]{1,0:T(8,128)} %bitcast.22, f32[1944,128]{1,0:T(8,128)} %bitcast.17, f32[1944,128]{1,0:T(8,128)} %bitcast.18, ...), custom_call_target="tpu_custom_call" | custom-call | tf_op jit(solution)/shard_map/exchange_and_rotate/pallas_call | solution.py:681
  81.0 4.0 %unpack.1 = (f32[1944,128]{1,0:T(8,128)}, f32[1944,128]{1,0:T(8,128)}, f32[1944,128]{1,0:T(8,128)}, f32[2,96,384]{2,1,0:T(8,128)}, f32[2,96,384]{2,1,0:T(8,128)}...) custom-call(s32[128]{0:T(128)} %get-tuple-element.22.places, f32[2304,128]{1,0:T(8,128)} %get-tuple-element.23.back_d, ...), custom_call_target="tpu_custom_call" | custom-call | tf_op jit(solution)/shard_map/unpack/pallas_call | solution.py:717
